TPU v7x, 32 devices: a whole 2x2x4 slice. The times are simulated.
32 devices in a mesh: seq: 16 (over z, x, core), head: 2 (over y).
Axes of the slice: x: 2, y: 2, z: 4, core: 2. Of those that a mesh axis runs over, the one named last changes fastest.
Arguments:
- queries: bfloat16 [1, 4096, 8192], P(None, ('seq', 'head')), may hold values from -38 to 38
- keys: bfloat16 [1, 4096, 1024], P(None, ('seq', 'head')), may hold values from -6 to 6
- values: bfloat16 [1, 4096, 1024], P(None, ('seq', 'head')), may hold values from -6 to 6
- output_gradient: bfloat16 [1, 4096, 8192], P(None, ('seq', 'head')), may hold values from -6 to 6
- kv_blocks: int32 [32, 8], replicated, may hold values from -1 to 31, as said below
- block_position: int32 [32], replicated, may hold values from 0 to 31, as said below
Outputs:
- attention: bfloat16 [1, 4096, 8192], P(None, 'seq', 'head')
- query_grad: bfloat16 [1, 4096, 8192], P(None, 'seq', 'head')
- key_gradient: bfloat16 [1, 4096, 1024], P(None, 'seq', 'head')
- value_gradient: bfloat16 [1, 4096, 1024], P(None, 'seq', 'head')
Inputs may be any that keep to these rules, and one draw needn't show every extreme that they name: `block_position`: stored blocks 2d and 2d + 1 hold logical blocks k and 31 - k, for one k per d and each k once. `kv_blocks`: row p lists p, then p - 1 (-1 if p = 0), then each global block g < 2 if g < p - 1 (else -1), then up to 4 distinct blocks from 2 to p - 2 (-1 for missing ones). For logical blocks k and 31 - k together, the listed blocks of 2 or more that lie outside that pair lie in distinct pairs k2, 31 - k2, and each is listed once.
All inputs are finite; a program needn't handle non-finite values.
Results may differ from a plain program's by a relative error of at most 0.03.
Values may be sent and summed in bfloat16 or wider, within the bound.
No kernel may reach another device: no remote copies, remote signals or barrier semaphores. Data moves between devices by JAX's collectives and lax.ppermute only.
A program may use at most 192 MiB of HBM per device.

v0:
```python
import functools

import jax
import jax.numpy as jnp
from jax import lax
from jax.experimental import pallas as pl
from jax.experimental.pallas import tpu as pltpu
from jax.sharding import PartitionSpec as P


QUERY_HEADS = 64
KEY_VALUE_HEADS = 8
HEAD_SIZE = 128
BLOCK_TOKENS = 128
GROUP = QUERY_HEADS // KEY_VALUE_HEADS
GROUP_WIDTH = GROUP * HEAD_SIZE
HEADS_AT_ONCE = 4
LOG2E = 1.4426950408889634
FACTOR = HEAD_SIZE ** (-0.5)


NT = (((1,), (1,)), ((), ()))
TN = (((0,), (0,)), ((), ()))
NN = (((1,), (0,)), ((), ()))


def dot(a, b, dims):
    return lax.dot_general(a, b, dims, preferred_element_type=jnp.float32)


def stored_index(block_position):
    block_list = block_position.shape[0]
    stored = jnp.arange(block_list, dtype=jnp.int32)
    matches = block_position[None, :] == stored[:, None]
    return jnp.sum(jnp.where(matches, stored[None, :], 0), axis=1)


def attend_block(i, slot_ref, q_ref, g_ref, kv_ref, a_ref, dq_ref, total, keys_at, values_at, part, slots):
    b = BLOCK_TOKENS
    d = HEAD_SIZE
    rows = HEADS_AT_ONCE * b
    for e in range(slots):
        at = jnp.maximum(slot_ref[i * slots + e], 0)
        keys_at[e * b : (e + 1) * b, :] = kv_ref[at, :, :d]
        values_at[e * b : (e + 1) * b, :] = kv_ref[at, :, d:]
    bias = [
        jnp.where(slot_ref[i * slots + e] >= 0, 0.0, jnp.inf).astype(jnp.float32) for e in range(slots)
    ]
    part[...] = jnp.zeros_like(part)

    def heads(j, carry):
        spans = [pl.ds((j * HEADS_AT_ONCE + t) * d, d) for t in range(HEADS_AT_ONCE)]
        q = jnp.concatenate([q_ref[i, :, span] for span in spans], axis=0)
        g = jnp.concatenate([g_ref[i, :, span] for span in spans], axis=0)
        k = keys_at[...]
        v = values_at[...]
        s = dot(q, k, NT)
        column = lax.broadcasted_iota(jnp.int32, (rows, b), 1)
        row = lax.broadcasted_iota(jnp.int32, (rows, b), 0) & (b - 1)
        tiles = [jnp.where(column <= row, s[:, :b], -jnp.inf)]
        tiles += [s[:, e * b : (e + 1) * b] for e in range(1, slots)]
        high = tiles[0]
        for e in range(1, slots):
            high = jnp.maximum(high, tiles[e] - bias[e])
        high = jnp.max(high, axis=1, keepdims=True) * (FACTOR * LOG2E)
        powers = [jnp.exp2(tiles[e] * (FACTOR * LOG2E) - (high + bias[e])) for e in range(slots)]
        inverse = 1.0 / jnp.sum(functools.reduce(jnp.add, powers), axis=1, keepdims=True)
        probs = jnp.concatenate([power * inverse for power in powers], axis=1)
        probs_half = probs.astype(jnp.bfloat16)
        out = dot(probs_half, v, NN).astype(jnp.bfloat16)
        dprobs = dot(g, v, NT)
        delta = jnp.sum(g.astype(jnp.float32) * out.astype(jnp.float32), axis=1, keepdims=True)
        dscores = (probs * (dprobs - delta)).astype(jnp.bfloat16)
        dq = (dot(dscores, k, NN) * FACTOR).astype(jnp.bfloat16)
        part[:, :d] += dot(dscores, q, TN)
        part[:, d:] += dot(probs_half, g, TN)
        for t, span in enumerate(spans):
            a_ref[i, :, span] = out[t * b : (t + 1) * b]
            dq_ref[i, :, span] = dq[t * b : (t + 1) * b]
        return carry

    lax.fori_loop(0, GROUP // HEADS_AT_ONCE, heads, 0)
    for e in range(slots):
        at = jnp.maximum(slot_ref[i * slots + e], 0)
        total[at, :, :d] += part[e * b : (e + 1) * b, :d] * FACTOR
        total[at, :, d:] += part[e * b : (e + 1) * b, d:]


def cost(blocks, slots, stored, wide):
    return pl.CostEstimate(
        flops=10 * blocks * slots * GROUP * BLOCK_TOKENS * BLOCK_TOKENS * HEAD_SIZE,
        transcendentals=blocks * slots * GROUP * BLOCK_TOKENS * BLOCK_TOKENS,
        bytes_accessed=blocks * BLOCK_TOKENS * GROUP_WIDTH * 8
        + stored * BLOCK_TOKENS * 2 * HEAD_SIZE * (2 + wide),
    )


def scratch(slots):
    return [
        pltpu.VMEM((slots * BLOCK_TOKENS, HEAD_SIZE), jnp.bfloat16),
        pltpu.VMEM((slots * BLOCK_TOKENS, HEAD_SIZE), jnp.bfloat16),
        pltpu.VMEM((slots * BLOCK_TOKENS, 2 * HEAD_SIZE), jnp.float32),
    ]


def plain_kernel(slot_ref, q_ref, g_ref, kv_ref, a_ref, dq_ref, total, keys_at, values_at, part, *, slots):
    total[...] = jnp.zeros_like(total)

    def block(i, carry):
        attend_block(i, slot_ref, q_ref, g_ref, kv_ref, a_ref, dq_ref, total, keys_at, values_at, part, slots)
        return carry

    lax.fori_loop(0, q_ref.shape[0], block, 0)


def plain_attention(slot, q, g, kv, slots):
    whole = pl.BlockSpec(memory_space=pltpu.VMEM)
    like = jax.ShapeDtypeStruct(q.shape, jnp.bfloat16)
    return pl.pallas_call(
        functools.partial(plain_kernel, slots=slots),
        grid_spec=pltpu.PrefetchScalarGridSpec(
            num_scalar_prefetch=1,
            grid=(),
            in_specs=[whole] * 3,
            out_specs=[whole] * 3,
            scratch_shapes=scratch(slots),
        ),
        out_shape=[like, like, jax.ShapeDtypeStruct(kv.shape, jnp.float32)],
        compiler_params=pltpu.CompilerParams(vmem_limit_bytes=60 << 20),
        cost_estimate=cost(q.shape[0], slots, kv.shape[0], 4),
    )(slot, q, g, kv)


def general(queries, keys, values, output_gradient, kv_blocks, block_position):
    query_home, key_home, value_home, grad_home = (
        lax.all_to_all(a, "head", split_axis=2, concat_axis=1, tiled=True)
        for a in (queries, keys, values, output_gradient)
    )
    sequences, tokens, _ = query_home.shape
    kv_heads = key_home.shape[2] // HEAD_SIZE
    per_device = tokens // BLOCK_TOKENS
    slots = kv_blocks.shape[1]
    my_index = lax.axis_index("seq")
    located = stored_index(block_position)
    my_blocks = lax.dynamic_slice_in_dim(block_position, my_index * per_device, per_device)
    listed = jnp.take(kv_blocks, my_blocks, axis=0).reshape(-1)
    slot = jnp.where(listed >= 0, jnp.take(located, jnp.maximum(listed, 0)), -1)
    outs = []
    for sequence in range(sequences):
        heads = []
        for head in range(kv_heads):
            wide = slice(head * GROUP_WIDTH, (head + 1) * GROUP_WIDTH)
            narrow = slice(head * HEAD_SIZE, (head + 1) * HEAD_SIZE)
            kv = jnp.concatenate([key_home[sequence, :, narrow], value_home[sequence, :, narrow]], axis=1)
            kv = lax.all_gather(kv, "seq", axis=0, tiled=True)
            kv = kv.reshape(-1, BLOCK_TOKENS, 2 * HEAD_SIZE)
            q = query_home[sequence, :, wide].reshape(per_device, BLOCK_TOKENS, GROUP_WIDTH)
            g = grad_home[sequence, :, wide].reshape(per_device, BLOCK_TOKENS, GROUP_WIDTH)
            attention, query_grad, total = plain_attention(slot, q, g, kv, slots)
            total = lax.psum_scatter(total, "seq", scatter_dimension=0, tiled=True)
            total = total.astype(jnp.bfloat16).reshape(tokens, 2 * HEAD_SIZE)
            heads.append(
                (
                    attention.reshape(tokens, GROUP_WIDTH),
                    query_grad.reshape(tokens, GROUP_WIDTH),
                    total[:, :HEAD_SIZE],
                    total[:, HEAD_SIZE:],
                )
            )
        outs.append(tuple(jnp.concatenate(parts, axis=1) for parts in zip(*heads)))
    return tuple(jnp.stack(parts) for parts in zip(*outs))


def quad_kernel(listed_ref, position_ref, q_ref, g_ref, *refs, slots, lines, kv_heads, head):
    pieces, refs = refs[:3], refs[3:]
    kv_line, kv_beside, a_own, dq_own, far, total_line, total_beside = refs[:7]
    located, slot, q_at, g_at, kv_at, a_at, dq_at, total, keys_at, values_at, part, kv_sem, in_sem, out_sem = refs[7:]
    s = lax.axis_index("seq")
    h = lax.axis_index("head")
    x = (s >> 1) & 1
    half = lines * 4
    fetches = [
        pltpu.make_async_copy(ref, kv_at.at[pl.ds(n * half, half)], kv_sem.at[n])
        for n, ref in enumerate((kv_line, kv_beside))
    ]
    column = (h * 2 + x) * kv_heads + head
    span = pl.ds(pl.multiple_of(column * GROUP_WIDTH, GROUP_WIDTH), GROUP_WIDTH)
    for which, (ref, at) in enumerate(((q_ref, q_at), (g_ref, g_at))):
        fetches.append(pltpu.make_async_copy(ref.at[0, :, span], at.at[0], in_sem.at[which, 0]))
        for n in range(3):
            fetches.append(pltpu.make_async_copy(pieces[n].at[which], at.at[n + 1], in_sem.at[which, n + 1]))
    for fetch in fetches:
        fetch.start()

    def locate(j, carry):
        located[position_ref[j]] = j
        return carry

    lax.fori_loop(0, lines * 8, locate, 0)

    def entry(n, carry):
        i, e = n // slots, n % slots
        stored = ((s ^ (2 * (i >> 1))) * 2) + (h ^ (i & 1))
        b = listed_ref[position_ref[stored], e]
        home = located[jnp.maximum(b, 0)]
        seq_home = home >> 1
        where_ = ((seq_home ^ s) & 1) * half + (seq_home >> 2) * 4
        where_ = where_ + (((seq_home >> 1) & 1) ^ x) * 2 + ((home & 1) ^ h)
        slot[n] = jnp.where(b >= 0, where_, -1)
        return carry

    lax.fori_loop(0, 4 * slots, entry, 0)
    total[...] = jnp.zeros_like(total)
    for fetch in fetches:
        fetch.wait()

    def block(i, carry):
        attend_block(i, slot, q_at, g_at, kv_at, a_at, dq_at, total, keys_at, values_at, part, slots)
        row = pl.ds(pl.multiple_of((h ^ (i & 1)) * BLOCK_TOKENS, BLOCK_TOKENS), BLOCK_TOKENS)

        @pl.when(i < 2)
        def _():
            pltpu.make_async_copy(a_at.at[i], a_own.at[row], out_sem.at[0]).start()
            pltpu.make_async_copy(dq_at.at[i], dq_own.at[row], out_sem.at[1]).start()

        @pl.when(i >= 2)
        def _():
            pltpu.make_async_copy(a_at.at[i], far.at[0, row], out_sem.at[2]).start()
            pltpu.make_async_copy(dq_at.at[i], far.at[1, row], out_sem.at[2]).start()

        return carry

    lax.fori_loop(0, 4, block, 0)
    total_line[...] = total[:half].astype(jnp.bfloat16)
    total_beside[...] = total[half:].astype(jnp.bfloat16)
    for n, ref in enumerate((a_own, dq_own, far)):
        pltpu.make_async_copy(ref, ref, out_sem.at[n]).wait()


def quad_attention(kv_blocks, block_position, queries, output_gradient, pieces, kv_line, kv_beside, lines, kv_heads, head):
    outside = pl.BlockSpec(memory_space=pltpu.HBM)
    inside = pl.BlockSpec(memory_space=pltpu.VMEM)
    slots = kv_blocks.shape[1]
    half = lines * 4
    own = jax.ShapeDtypeStruct((2 * BLOCK_TOKENS, GROUP_WIDTH), jnp.bfloat16)
    sums = jax.ShapeDtypeStruct((half, BLOCK_TOKENS, 2 * HEAD_SIZE), jnp.bfloat16)
    wide = pltpu.VMEM((4, BLOCK_TOKENS, GROUP_WIDTH), jnp.bfloat16)
    return pl.pallas_call(
        functools.partial(quad_kernel, slots=slots, lines=lines, kv_heads=kv_heads, head=head),
        grid_spec=pltpu.PrefetchScalarGridSpec(
            num_scalar_prefetch=2,
            grid=(),
            in_specs=[outside] * 7,
            out_specs=[outside] * 3 + [inside] * 2,
            scratch_shapes=[
                pltpu.SMEM((lines * 8,), jnp.int32),
                pltpu.SMEM((4 * slots,), jnp.int32),
                wide,
                wide,
                pltpu.VMEM((2 * half, BLOCK_TOKENS, 2 * HEAD_SIZE), jnp.bfloat16),
                wide,
                wide,
                pltpu.VMEM((2 * half, BLOCK_TOKENS, 2 * HEAD_SIZE), jnp.float32),
                *scratch(slots),
                pltpu.SemaphoreType.DMA((2,)),
                pltpu.SemaphoreType.DMA((2, 4)),
                pltpu.SemaphoreType.DMA((3,)),
            ],
        ),
        out_shape=[own, own, jax.ShapeDtypeStruct((2, *own.shape), jnp.bfloat16), sums, sums],
        compiler_params=pltpu.CompilerParams(vmem_limit_bytes=60 << 20),
        cost_estimate=cost(4, slots, 2 * half, 2),
    )(kv_blocks, block_position, queries, output_gradient, *pieces, kv_line, kv_beside)


def pack_kernel(keys_ref, values_ref, *outs, kv_heads):
    h = lax.axis_index("head")
    x = (lax.axis_index("seq") >> 1) & 1
    for n, out in enumerate(outs):
        quarter = (h ^ (n & 1)) * 2 + (x ^ (n >> 1))
        for head in range(kv_heads):
            start = (quarter * kv_heads + head) * HEAD_SIZE
            span = pl.ds(pl.multiple_of(start, HEAD_SIZE), HEAD_SIZE)
            out[head, :, :HEAD_SIZE] = keys_ref[0, :, span]
            out[head, :, HEAD_SIZE:] = values_ref[0, :, span]


def pack(keys, values, kv_heads):
    inside = pl.BlockSpec(memory_space=pltpu.VMEM)
    shape = jax.ShapeDtypeStruct((kv_heads, BLOCK_TOKENS, 2 * HEAD_SIZE), jnp.bfloat16)
    return pl.pallas_call(
        functools.partial(pack_kernel, kv_heads=kv_heads),
        in_specs=[inside] * 2,
        out_specs=[inside] * 4,
        out_shape=[shape] * 4,
    )(keys, values)


def pack_wide_kernel(q_ref, g_ref, *refs, kv_heads, head):
    outs, (held, in_sem, out_sem) = refs[:3], refs[3:]
    h = lax.axis_index("head")
    x = (lax.axis_index("seq") >> 1) & 1
    fetches = []
    for n in range(3):
        quarter = (h ^ ((n + 1) & 1)) * 2 + (x ^ ((n + 1) >> 1))
        start = (quarter * kv_heads + head) * GROUP_WIDTH
        span = pl.ds(pl.multiple_of(start, GROUP_WIDTH), GROUP_WIDTH)
        for which, ref in enumerate((q_ref, g_ref)):
            fetches.append(pltpu.make_async_copy(ref.at[0, :, span], held.at[n, which], in_sem.at[n, which]))
    for fetch in fetches:
        fetch.start()
    stores = []
    for n in range(3):
        fetches[2 * n].wait()
        fetches[2 * n + 1].wait()
        stores.append(pltpu.make_async_copy(held.at[n], outs[n], out_sem.at[n]))
        stores[n].start()
    for store in stores:
        store.wait()


def pack_wide(queries, output_gradient, kv_heads, head):
    outside = pl.BlockSpec(memory_space=pltpu.HBM)
    shape = jax.ShapeDtypeStruct((2, BLOCK_TOKENS, GROUP_WIDTH), jnp.bfloat16)
    return pl.pallas_call(
        functools.partial(pack_wide_kernel, kv_heads=kv_heads, head=head),
        in_specs=[outside] * 2,
        out_specs=[outside] * 3,
        out_shape=[shape] * 3,
        scratch_shapes=[
            pltpu.VMEM((3, *shape.shape), jnp.bfloat16),
            pltpu.SemaphoreType.DMA((3, 2)),
            pltpu.SemaphoreType.DMA((3,)),
        ],
        cost_estimate=pl.CostEstimate(flops=0, transcendentals=0, bytes_accessed=12 * BLOCK_TOKENS * GROUP_WIDTH * 2),
    )(queries, output_gradient)


def spread_kernel(*refs, head):
    out = refs[-1]
    for line in range(out.shape[0] // 4):
        for n in range(4):
            out[line * 4 + n] = refs[n][head]


def spread(parts, head, lines):
    inside = pl.BlockSpec(memory_space=pltpu.VMEM)
    return pl.pallas_call(
        functools.partial(spread_kernel, head=head),
        in_specs=[inside] * 4,
        out_specs=inside,
        out_shape=jax.ShapeDtypeStruct((lines * 4, BLOCK_TOKENS, 2 * HEAD_SIZE), jnp.bfloat16),
    )(*parts)


def quad(queries, keys, values, output_gradient, kv_blocks, block_position):
    seq_count = lax.axis_size("seq")
    lines = seq_count // 4
    s = lax.axis_index("seq")
    h = lax.axis_index("head")
    x = (s // 2) % 2
    kv_heads = keys.shape[2] // HEAD_SIZE // 4
    across = [(0, 1), (1, 0)]
    beside = [(i, i ^ 1) for i in range(seq_count)]
    sideways = [(i, i ^ 2) for i in range(seq_count)]
    corner = [(i * 2 + j, (i ^ 2) * 2 + 1 - j) for i in range(seq_count) for j in range(2)]
    line_groups = [[line * 4 + r for line in range(lines)] for r in range(4)]

    def trade(parts):
        return [
            lax.ppermute(parts[0], "head", across),
            lax.ppermute(parts[1], "seq", sideways),
            lax.ppermute(parts[2], ("seq", "head"), corner),
        ]

    def along_line(array):
        return lax.all_to_all(array, "seq", split_axis=0, concat_axis=0, tiled=True, axis_index_groups=line_groups)

    own, *others = pack(keys, values, kv_heads)
    kv_parts = [own] + trade(others)
    pieces = []
    for head in range(kv_heads):
        parts = pack_wide(queries, output_gradient, kv_heads, head)
        pieces.append(trade(parts))
    kv_lines = []
    for head in range(kv_heads):
        copies = spread(kv_parts, head, lines)
        kv_lines.append(along_line(copies))
    own_parts = []
    far_parts = []
    grad_parts = []
    for head in range(kv_heads):
        kv_beside = lax.ppermute(kv_lines[head], "seq", beside)
        a_own, dq_own, far, total_line, total_beside = quad_attention(
            kv_blocks, block_position, queries, output_gradient, pieces[head], kv_lines[head], kv_beside, lines, kv_heads, head
        )
        arrived = lax.ppermute(total_beside, "seq", beside)
        far_parts.append(lax.ppermute(far, "seq", sideways))
        own_parts.append((a_own, dq_own))
        total = total_line.astype(jnp.float32) + arrived.astype(jnp.float32)
        returned = along_line(total.astype(jnp.bfloat16))
        returned = returned.reshape(lines, 2, 2, BLOCK_TOKENS, 2 * HEAD_SIZE)
        summed = jnp.sum(returned.astype(jnp.float32), axis=0).astype(jnp.bfloat16)
        grad_parts.append((summed[0], lax.ppermute(summed[1], "seq", sideways)))

    def place(own, far):
        return jnp.where(x == 0, jnp.concatenate(own + far, axis=-1), jnp.concatenate(far + own, axis=-1))

    outs = [place([part[n] for part in own_parts], [part[n] for part in far_parts])[None] for n in range(2)]
    for n in range(2):
        span = slice(n * HEAD_SIZE, (n + 1) * HEAD_SIZE)
        grad = place([part[0][..., span] for part in grad_parts], [part[1][..., span] for part in grad_parts])
        grad = jnp.where(h == 0, grad, grad[::-1])
        outs.append(grad.reshape(1, 2 * BLOCK_TOKENS, -1))
    return tuple(outs)


def body(queries, keys, values, output_gradient, kv_blocks, block_position):
    sequences, tokens, _ = queries.shape
    fits = (
        lax.axis_size("head") == 2
        and lax.axis_size("seq") % 4 == 0
        and sequences == 1
        and tokens == BLOCK_TOKENS
        and KEY_VALUE_HEADS % 4 == 0
    )
    chosen = quad if fits else general
    return chosen(queries, keys, values, output_gradient, kv_blocks, block_position)


def solution(mesh):
    placed = (
        P(None, ("seq", "head"), None),
        P(None, ("seq", "head"), None),
        P(None, ("seq", "head"), None),
        P(None, ("seq", "head"), None),
        P(),
        P(),
    )
    return jax.shard_map(
        body,
        mesh=mesh,
        in_specs=placed,
        out_specs=(
            P(None, "seq", "head"),
            P(None, "seq", "head"),
            P(None, "seq", "head"),
            P(None, "seq", "head"),
        ),
        check_vma=False,
    )
```

profile of v0, /device:TPU:0, one launch (start us, length us, event | category | flops | bytes accessed | tf_op | source)
XLA Modules:
  0.0 226.2 jit_solution(10963529544145649086)
XLA Ops:
  0.6 1.9 shard_map.94
  2.6 3.0 %collective-permute-start.3 = (bf16[2,128,256]{2,1,0:T(8,128)(2,1)}, bf16[2,128,256]{2,1,0:T(8,128)(2,1)S(1)}, u32[]{:S(2)}, u32[]{:S(2)}) collective-permute-start(bf16[2,128,256]{2,1,0:T(8,128)(2,1)} %get-tuple-element.28), channel_id=1, source_target_pairs={{0,1},{1,0},{2,3},{3,2},{4,5},{5,4},{6,7},{7,6},{8,9},{9,8},{10,11... | collective-permute-start | bytes 393224 | tf_op jit(solution)/shard_map/ppermute | solution.py:371
  5.6 1.5 collective-permute-start.4
  7.1 0.0 collective-permute-start.5
  7.1 2.2 collective-permute-done.3.refs_1_
  9.3 2.9 %collective-permute-done.4.refs_2_ = bf16[2,128,256]{2,1,0:T(8,128)(2,1)S(1)} collective-permute-done((bf16[2,128,256]{2,1,0:T(8,128)(2,1)}, bf16[2,128,256]{2,1,0:T(8,128)(2,1)S(1)}, u32[]{:S(2)}, u32[]{:S(2)}) %collective-permute-start.4) | collective-permute-done | bytes 131104 | tf_op jit(solution)/shard_map/ppermute | solution.py:372
  12.2 1.1 collective-permute-done.5.refs_3_
  13.3 0.0 copy-done.8
  13.3 0.6 copy-done.9
  13.9 2.1 shard_map.95
  16.1 30.1 %all_to_all.20.refs_3_ = bf16[16,128,256]{2,1,0:T(8,128)(2,1)S(1)} all-to-all(bf16[16,128,256]{2,1,0:T(8,128)(2,1)} %shard_map.95), channel_id=1, replica_groups={{0,8,16,24},{2,10,18,26},{4,12,20,28},{6,14,22,30},{1,9,17,25},{3,11,19..., dimensions={0} | all-to-all | bytes 2097152 | tf_op jit(solution)/shard_map/all_to_all | solution.py:377
  46.1 0.0 collective-permute-start.6
  46.1 2.5 %shard_map.98 = bf16[16,128,256]{2,1,0:T(8,128)(2,1)} custom-call(bf16[2,128,256]{2,1,0:T(8,128)(2,1)} %get-tuple-element.27.refs_0_, bf16[2,128,256]{2,1,0:T(8,128)(2,1)} %copy-done.7, bf16[2,128,256]{2,1,0:T(8,128)(2,1)} %copy-done.8, bf16[2,128,256]{2,1,0:T(8,128)(2,1)} %copy-done.9), custom_call_target="tpu_custom_call" | custom-call | tf_op jit(solution)/shard_map/pallas_call | solution.py:348
  48.6 3.5 %all-to-all-start.1 = ((bf16[16,128,256]{2,1,0:T(8,128)(2,1)}), bf16[16,128,256]{2,1,0:T(8,128)(2,1)S(1)}, u32[]{:S(2)}, u32[]{:S(2)}) async-start(bf16[16,128,256]{2,1,0:T(8,128)(2,1)} %shard_map.98), calls=%async_computation.1 | async-start | bytes 2097152 | tf_op jit(solution)/shard_map/all_to_all | solution.py:377
  52.2 0.0 copy-start.10
  52.2 2.3 %shard_map.93 = (bf16[2,128,1024]{2,1,0:T(8,128)(2,1)}, bf16[2,128,1024]{2,1,0:T(8,128)(2,1)}, bf16[2,128,1024]{2,1,0:T(8,128)(2,1)}) custom-call(bf16[1,128,8192]{2,1,0:T(8,128)(2,1)} %q_ref.7, bf16[1,128,8192]{2,1,0:T(8,128)(2,1)} %g_ref.7), custom_call_target="tpu_custom_call" | custom-call | bytes 3145728 | tf_op jit(solution)/shard_map/pallas_call | solution.py:325
  54.5 0.9 collective-permute-start
  55.4 1.5 collective-permute-start.1
  56.9 1.1 collective-permute-start.2
  58.0 0.7 copy.10.listed_ref
  58.7 10.1 %collective-permute-done.refs_0_ = bf16[2,128,1024]{2,1,0:T(8,128)(2,1)} collective-permute-done((bf16[2,128,1024]{2,1,0:T(8,128)(2,1)}, bf16[2,128,1024]{2,1,0:T(8,128)(2,1)}, u32[]{:S(2)}, u32[]{:S(2)}) %collective-permute-start) | collective-permute-done | bytes 524320 | tf_op jit(solution)/shard_map/ppermute | solution.py:371
  68.8 1.7 collective-permute-done.1.refs_1_
  70.5 10.7 %collective-permute-done.2.refs_2_ = bf16[2,128,1024]{2,1,0:T(8,128)(2,1)} collective-permute-done((bf16[2,128,1024]{2,1,0:T(8,128)(2,1)}, bf16[2,128,1024]{2,1,0:T(8,128)(2,1)}, u32[]{:S(2)}, u32[]{:S(2)}) %collective-permute-start.2) | collective-permute-done | bytes 524320 | tf_op jit(solution)/shard_map/ppermute | solution.py:373
  81.2 0.0 collective-permute-done.6.refs_4_
  81.2 1.0 copy-done.11
  82.2 26.5 %shard_map.96 = (bf16[256,1024]{1,0:T(8,128)(2,1)}, bf16[256,1024]{1,0:T(8,128)(2,1)}, bf16[2,256,1024]{2,1,0:T(8,128)(2,1)}, bf16[16,128,256]{2,1,0:T(8,128)(2,1)}, bf16[16,128,256]{2,1,0:T(8,128)(2,1)}) custom-call(s32[32,8]{1,0:T(8,128)} %copy.10.listed_ref, s32[32]{0:T(128)} %position_ref.3, bf16[1,128,8192]{2,1,0:T(8,128)(2,1)} %q_ref.7, ...), custom_call_target="tpu_custom_call" | custom-call | flops 5368709120 | bytes 8388608 | tf_op jit(solution)/shard_map/pallas_call | solution.py:248
  108.7 0.1 collective-permute-start.13
  108.8 0.0 all-to-all-done.1.refs_3_
  108.8 0.0 copy-start.1
  108.8 0.5 collective-permute-start.10
  109.3 2.4 %shard_map.97 = (bf16[2,128,1024]{2,1,0:T(8,128)(2,1)}, bf16[2,128,1024]{2,1,0:T(8,128)(2,1)}, bf16[2,128,1024]{2,1,0:T(8,128)(2,1)}) custom-call(bf16[1,128,8192]{2,1,0:T(8,128)(2,1)} %q_ref.7, bf16[1,128,8192]{2,1,0:T(8,128)(2,1)} %g_ref.7), custom_call_target="tpu_custom_call" | custom-call | bytes 3145728 | tf_op jit(solution)/shard_map/pallas_call | solution.py:325
  111.7 0.9 collective-permute-start.7
  112.7 1.5 collective-permute-start.8
  114.1 1.1 collective-permute-start.9
  115.3 0.0 collective-permute-done.13
  115.3 1.3 add_convert_fusion.1
  116.6 4.8 %all-to-all-start.2 = ((bf16[16,128,256]{2,1,0:T(8,128)(2,1)}), bf16[16,128,256]{2,1,0:T(8,128)(2,1)S(1)}, u32[]{:S(2)}, u32[]{:S(2)}) async-start(bf16[16,128,256]{2,1,0:T(8,128)(2,1)} %add_convert_fusion.1), calls=%async_computation.2 | async-start | bytes 2097152 | tf_op jit(solution)/shard_map/all_to_all | solution.py:377
  121.3 4.9 %collective-permute-done.7.refs_0_ = bf16[2,128,1024]{2,1,0:T(8,128)(2,1)} collective-permute-done((bf16[2,128,1024]{2,1,0:T(8,128)(2,1)}, bf16[2,128,1024]{2,1,0:T(8,128)(2,1)}, u32[]{:S(2)}, u32[]{:S(2)}) %collective-permute-start.7) | collective-permute-done | bytes 524320 | tf_op jit(solution)/shard_map/ppermute | solution.py:371
  126.2 1.6 collective-permute-done.8.refs_1_
  127.8 10.9 %collective-permute-done.9.refs_2_ = bf16[2,128,1024]{2,1,0:T(8,128)(2,1)} collective-permute-done((bf16[2,128,1024]{2,1,0:T(8,128)(2,1)}, bf16[2,128,1024]{2,1,0:T(8,128)(2,1)}, u32[]{:S(2)}, u32[]{:S(2)}) %collective-permute-start.9) | collective-permute-done | bytes 524320 | tf_op jit(solution)/shard_map/ppermute | solution.py:373
  138.6 0.0 collective-permute-done.10.refs_4_
  138.6 26.5 %shard_map.99 = (bf16[256,1024]{1,0:T(8,128)(2,1)}, bf16[256,1024]{1,0:T(8,128)(2,1)}, bf16[2,256,1024]{2,1,0:T(8,128)(2,1)}, bf16[16,128,256]{2,1,0:T(8,128)(2,1)}, bf16[16,128,256]{2,1,0:T(8,128)(2,1)}) custom-call(s32[32,8]{1,0:T(8,128)} %copy.10.listed_ref, s32[32]{0:T(128)} %position_ref.3, bf16[1,128,8192]{2,1,0:T(8,128)(2,1)} %q_ref.7, ...), custom_call_target="tpu_custom_call" | custom-call | flops 5368709120 | bytes 8388608 | tf_op jit(solution)/shard_map/pallas_call | solution.py:248
  165.1 0.1 collective-permute-start.14
  165.2 0.9 collective-permute-start.11
  166.1 1.2 collective-permute-start.12
  167.3 0.8 collective-permute-done.14
  168.0 2.5 %add_convert_fusion = bf16[16,128,256]{2,1,0:T(8,128)(2,1)} fusion(bf16[16,128,256]{2,1,0:T(8,128)(2,1)S(1)} %collective-permute-done.14, bf16[16,128,256]{2,1,0:T(8,128)(2,1)} %get-tuple-element.42), kind=kLoop, calls=%fused_computation.2 | loop fusion | flops 2097152 | bytes 3145728 | tf_op jit(solution)/shard_map/convert_element_type | solution.py:401
  170.6 0.0 all-to-all-done.2
  170.6 4.8 %all-to-all-start.3 = ((bf16[16,128,256]{2,1,0:T(8,128)(2,1)}), bf16[16,128,256]{2,1,0:T(8,128)(2,1)S(1)}, u32[]{:S(2)}, u32[]{:S(2)}) async-start(bf16[16,128,256]{2,1,0:T(8,128)(2,1)} %add_convert_fusion), calls=%async_computation.3 | async-start | bytes 2097152 | tf_op jit(solution)/shard_map/all_to_all | solution.py:377
  175.4 16.2 %collective-permute-done.11 = bf16[2,256,1024]{2,1,0:T(8,128)(2,1)} collective-permute-done((bf16[2,256,1024]{2,1,0:T(8,128)(2,1)}, bf16[2,256,1024]{2,1,0:T(8,128)(2,1)}, u32[]{:S(2)}, u32[]{:S(2)}) %collective-permute-start.11) | collective-permute-done | bytes 1048608 | tf_op jit(solution)/shard_map/ppermute | solution.py:398
  191.6 1.3 fusion
  192.9 20.6 %collective-permute-done.12 = bf16[2,256,1024]{2,1,0:T(8,128)(2,1)S(1)} collective-permute-done((bf16[2,256,1024]{2,1,0:T(8,128)(2,1)}, bf16[2,256,1024]{2,1,0:T(8,128)(2,1)S(1)}, u32[]{:S(2)}, u32[]{:S(2)}) %collective-permute-start.12) | collective-permute-done | bytes 1048608 | tf_op jit(solution)/shard_map/ppermute | solution.py:398
  213.4 0.1 fusion.1
  213.5 2.8 %maximum_select_fusion = (bf16[1,256,4096]{2,1,0:T(8,128)(2,1)}, bf16[1,256,4096]{2,1,0:T(8,128)(2,1)}) fusion(bf16[1,256,1024]{2,1,0:T(8,128)(2,1)S(1)} %get-tuple-element.47, bf16[1,256,1024]{2,1,0:T(8,128)(2,1)S(1)} %get-tuple-element.45, bf16[1,256,1024]{2,1,0:T(8,128)(2,1)S(1)} %bitcast.20, bf16[1,256,1024]{2,1,0:T(8,128)(2,1)S(1)} %bitcast.18, ...), kind=kLoop, calls=%fused_computation | loop fusion | flops 35651584 | bytes 8388609 | tf_op jit(solution)/shard_map/jit(_where)/select_n | solution.py:407
  216.3 0.2 reduce_sum.24
  216.6 0.9 collective-permute-start.15
  217.5 0.0 all-to-all-done.3
  217.5 0.2 reduce_sum.25
  217.8 1.3 collective-permute-start.16
  219.1 4.0 %collective-permute-done.15 = bf16[2,128,256]{2,1,0:T(8,128)(2,1)S(1)} collective-permute-done((bf16[2,128,256]{2,1,0:T(8,128)(2,1)S(1)}, bf16[2,128,256]{2,1,0:T(8,128)(2,1)S(1)}, u32[]{:S(2)}, u32[]{:S(2)}) %collective-permute-start.15) | collective-permute-done | bytes 131104 | tf_op jit(solution)/shard_map/ppermute | solution.py:404
  223.0 1.4 collective-permute-done.16
  224.5 0.2 maximum_select_fusion.2
  224.7 0.8 reverse_select_fusion
  225.4 0.7 reverse_select_fusion.1
  (25 shorter events, 0.2 us)
Async XLA Ops:
  2.6 6.7 %collective-permute-start.3 = (bf16[2,128,256]{2,1,0:T(8,128)(2,1)}, bf16[2,128,256]{2,1,0:T(8,128)(2,1)S(1)}, u32[]{:S(2)}, u32[]{:S(2)}) collective-permute-start(bf16[2,128,256]{2,1,0:T(8,128)(2,1)} %get-tuple-element.28), channel_id=1, source_target_pairs={{0,1},{1,0},{2,3},{3,2},{4,5},{5,4},{6,7},{7,6},{8,9},{9,8},{10,11... | collective-permute-start | bytes 393224 | tf_op jit(solution)/shard_map/ppermute | solution.py:371
  5.6 6.6 %collective-permute-start.4 = (bf16[2,128,256]{2,1,0:T(8,128)(2,1)}, bf16[2,128,256]{2,1,0:T(8,128)(2,1)S(1)}, u32[]{:S(2)}, u32[]{:S(2)}) collective-permute-start(bf16[2,128,256]{2,1,0:T(8,128)(2,1)} %get-tuple-element.29), channel_id=1, source_target_pairs={{0,4},{2,6},{4,0},{6,2},{8,12},{10,14},{12,8},{14,10},{16,20},{18,... | collective-permute-start | bytes 393224 | tf_op jit(solution)/shard_map/ppermute | solution.py:372
  7.1 6.2 %collective-permute-start.5 = (bf16[2,128,256]{2,1,0:T(8,128)(2,1)}, bf16[2,128,256]{2,1,0:T(8,128)(2,1)S(1)}, u32[]{:S(2)}, u32[]{:S(2)}) collective-permute-start(bf16[2,128,256]{2,1,0:T(8,128)(2,1)} %get-tuple-element.30), channel_id=1, source_target_pairs={{0,5},{1,4},{2,7},{3,6},{4,1},{5,0},{6,3},{7,2},{8,13},{9,12},{10,... | collective-permute-start | bytes 393224 | tf_op jit(solution)/shard_map/ppermute | solution.py:373
  9.3 4.0 %copy-start.7 = (bf16[2,128,256]{2,1,0:T(8,128)(2,1)}, bf16[2,128,256]{2,1,0:T(8,128)(2,1)S(1)}, u32[]{:S(2)}) copy-start(bf16[2,128,256]{2,1,0:T(8,128)(2,1)S(1)} %collective-permute-done.3.refs_1_) | copy-start | bytes 393220
  12.1 1.1 copy-start.8
  13.3 0.7 copy-start.9
  46.1 8.4 %copy-start.2 = (bf16[16,128,256]{2,1,0:T(8,128)(2,1)}, bf16[16,128,256]{2,1,0:T(8,128)(2,1)S(1)}, u32[]{:S(2)}) copy-start(bf16[16,128,256]{2,1,0:T(8,128)(2,1)S(1)} %all_to_all.20.refs_3_) | copy-start | bytes 3145732
  46.1 35.1 %collective-permute-start.6 = (bf16[16,128,256]{2,1,0:T(8,128)(2,1)S(1)}, bf16[16,128,256]{2,1,0:T(8,128)(2,1)S(1)}, u32[]{:S(2)}, u32[]{:S(2)}) collective-permute-start(bf16[16,128,256]{2,1,0:T(8,128)(2,1)S(1)} %all_to_all.20.refs_3_), channel_id=1, source_target_pairs={{0,2},{2,0},{4,6},{6,4},{8,10},{10,8},{12,14},{14,12},{16,18},{18,... | collective-permute-start | bytes 3145736 | tf_op jit(solution)/shard_map/ppermute | solution.py:393
  48.6 60.2 %all-to-all-start.1 = ((bf16[16,128,256]{2,1,0:T(8,128)(2,1)}), bf16[16,128,256]{2,1,0:T(8,128)(2,1)S(1)}, u32[]{:S(2)}, u32[]{:S(2)}) async-start(bf16[16,128,256]{2,1,0:T(8,128)(2,1)} %shard_map.98), calls=%async_computation.1 | async-start | bytes 2097152 | tf_op jit(solution)/shard_map/all_to_all | solution.py:377
  52.2 5.9 %copy-start.10 = (s32[32,8]{0,1:T(8,128)S(1)}, s32[32,8]{0,1:T(8,128)}, u32[]{:S(2)}) copy-start(s32[32,8]{0,1:T(8,128)} %param.10) | copy-start | bytes 3076
  54.5 14.3 %collective-permute-start = (bf16[2,128,1024]{2,1,0:T(8,128)(2,1)}, bf16[2,128,1024]{2,1,0:T(8,128)(2,1)}, u32[]{:S(2)}, u32[]{:S(2)}) collective-permute-start(bf16[2,128,1024]{2,1,0:T(8,128)(2,1)} %get-tuple-element.24), channel_id=1, source_target_pairs={{0,1},{1,0},{2,3},{3,2},{4,5},{5,4},{6,7},{7,6},{8,9},{9,8},{10,11... | collective-permute-start | bytes 1572872 | tf_op jit(solution)/shard_map/ppermute | solution.py:371
  55.4 15.1 %collective-permute-start.1 = (bf16[2,128,1024]{2,1,0:T(8,128)(2,1)}, bf16[2,128,1024]{2,1,0:T(8,128)(2,1)}, u32[]{:S(2)}, u32[]{:S(2)}) collective-permute-start(bf16[2,128,1024]{2,1,0:T(8,128)(2,1)} %get-tuple-element.25), channel_id=1, source_target_pairs={{0,4},{2,6},{4,0},{6,2},{8,12},{10,14},{12,8},{14,10},{16,20},{18,... | collective-permute-start | bytes 1572872 | tf_op jit(solution)/shard_map/ppermute | solution.py:372
  56.9 24.4 %collective-permute-start.2 = (bf16[2,128,1024]{2,1,0:T(8,128)(2,1)}, bf16[2,128,1024]{2,1,0:T(8,128)(2,1)}, u32[]{:S(2)}, u32[]{:S(2)}) collective-permute-start(bf16[2,128,1024]{2,1,0:T(8,128)(2,1)} %get-tuple-element.26), channel_id=1, source_target_pairs={{0,5},{1,4},{2,7},{3,6},{4,1},{5,0},{6,3},{7,2},{8,13},{9,12},{10,... | collective-permute-start | bytes 1572872 | tf_op jit(solution)/shard_map/ppermute | solution.py:373
  81.2 1.0 copy-start.11
  108.7 6.6 %copy-start = (bf16[16,128,256]{2,1,0:T(8,128)(2,1)S(1)}, bf16[16,128,256]{2,1,0:T(8,128)(2,1)}, u32[]{:S(2)}) copy-start(bf16[16,128,256]{2,1,0:T(8,128)(2,1)} %get-tuple-element.40) | copy-start | bytes 3145732
  108.7 6.6 %collective-permute-start.13 = (bf16[16,128,256]{2,1,0:T(8,128)(2,1)}, bf16[16,128,256]{2,1,0:T(8,128)(2,1)S(1)}, u32[]{:S(2)}, u32[]{:S(2)}) collective-permute-start(bf16[16,128,256]{2,1,0:T(8,128)(2,1)} %get-tuple-element.41), channel_id=1, source_target_pairs={{0,2},{2,0},{4,6},{6,4},{8,10},{10,8},{12,14},{14,12},{16,18},{18,... | collective-permute-start | bytes 3145736 | tf_op jit(solution)/shard_map/ppermute | solution.py:397
  108.8 2.9 %copy-start.1 = (bf16[16,128,256]{2,1,0:T(8,128)(2,1)}, bf16[16,128,256]{2,1,0:T(8,128)(2,1)S(1)}, u32[]{:S(2)}) copy-start(bf16[16,128,256]{2,1,0:T(8,128)(2,1)S(1)} %all-to-all-done.1.refs_3_) | copy-start | bytes 3145732
  108.8 29.8 %collective-permute-start.10 = (bf16[16,128,256]{2,1,0:T(8,128)(2,1)S(1)}, bf16[16,128,256]{2,1,0:T(8,128)(2,1)}, u32[]{:S(2)}, u32[]{:S(2)}) collective-permute-start(bf16[16,128,256]{2,1,0:T(8,128)(2,1)S(1)} %all-to-all-done.1.refs_3_), channel_id=1, source_target_pairs={{0,2},{2,0},{4,6},{6,4},{8,10},{10,8},{12,14},{14,12},{16,18},{18,... | collective-permute-start | bytes 3145736 | tf_op jit(solution)/shard_map/ppermute | solution.py:393
  111.7 14.5 %collective-permute-start.7 = (bf16[2,128,1024]{2,1,0:T(8,128)(2,1)}, bf16[2,128,1024]{2,1,0:T(8,128)(2,1)}, u32[]{:S(2)}, u32[]{:S(2)}) collective-permute-start(bf16[2,128,1024]{2,1,0:T(8,128)(2,1)} %get-tuple-element.32), channel_id=1, source_target_pairs={{0,1},{1,0},{2,3},{3,2},{4,5},{5,4},{6,7},{7,6},{8,9},{9,8},{10,11... | collective-permute-start | bytes 1572872 | tf_op jit(solution)/shard_map/ppermute | solution.py:371
  112.7 15.1 %collective-permute-start.8 = (bf16[2,128,1024]{2,1,0:T(8,128)(2,1)}, bf16[2,128,1024]{2,1,0:T(8,128)(2,1)}, u32[]{:S(2)}, u32[]{:S(2)}) collective-permute-start(bf16[2,128,1024]{2,1,0:T(8,128)(2,1)} %get-tuple-element.33), channel_id=1, source_target_pairs={{0,4},{2,6},{4,0},{6,2},{8,12},{10,14},{12,8},{14,10},{16,20},{18,... | collective-permute-start | bytes 1572872 | tf_op jit(solution)/shard_map/ppermute | solution.py:372
  114.1 24.5 %collective-permute-start.9 = (bf16[2,128,1024]{2,1,0:T(8,128)(2,1)}, bf16[2,128,1024]{2,1,0:T(8,128)(2,1)}, u32[]{:S(2)}, u32[]{:S(2)}) collective-permute-start(bf16[2,128,1024]{2,1,0:T(8,128)(2,1)} %get-tuple-element.34), channel_id=1, source_target_pairs={{0,5},{1,4},{2,7},{3,6},{4,1},{5,0},{6,3},{7,2},{8,13},{9,12},{10,... | collective-permute-start | bytes 1572872 | tf_op jit(solution)/shard_map/ppermute | solution.py:373
  116.6 54.0 %all-to-all-start.2 = ((bf16[16,128,256]{2,1,0:T(8,128)(2,1)}), bf16[16,128,256]{2,1,0:T(8,128)(2,1)S(1)}, u32[]{:S(2)}, u32[]{:S(2)}) async-start(bf16[16,128,256]{2,1,0:T(8,128)(2,1)} %add_convert_fusion.1), calls=%async_computation.2 | async-start | bytes 2097152 | tf_op jit(solution)/shard_map/all_to_all | solution.py:377
  165.1 2.9 %collective-permute-start.14 = (bf16[16,128,256]{2,1,0:T(8,128)(2,1)}, bf16[16,128,256]{2,1,0:T(8,128)(2,1)S(1)}, u32[]{:S(2)}, u32[]{:S(2)}) collective-permute-start(bf16[16,128,256]{2,1,0:T(8,128)(2,1)} %get-tuple-element.43), channel_id=1, source_target_pairs={{0,2},{2,0},{4,6},{6,4},{8,10},{10,8},{12,14},{14,12},{16,18},{18,... | collective-permute-start | bytes 3145736 | tf_op jit(solution)/shard_map/ppermute | solution.py:397
  165.2 26.4 %collective-permute-start.11 = (bf16[2,256,1024]{2,1,0:T(8,128)(2,1)}, bf16[2,256,1024]{2,1,0:T(8,128)(2,1)}, u32[]{:S(2)}, u32[]{:S(2)}) collective-permute-start(bf16[2,256,1024]{2,1,0:T(8,128)(2,1)} %get-tuple-element.36), channel_id=1, source_target_pairs={{0,4},{2,6},{4,0},{6,2},{8,12},{10,14},{12,8},{14,10},{16,20},{18,... | collective-permute-start | bytes 3145736 | tf_op jit(solution)/shard_map/ppermute | solution.py:398
  166.1 47.4 %collective-permute-start.12 = (bf16[2,256,1024]{2,1,0:T(8,128)(2,1)}, bf16[2,256,1024]{2,1,0:T(8,128)(2,1)S(1)}, u32[]{:S(2)}, u32[]{:S(2)}) collective-permute-start(bf16[2,256,1024]{2,1,0:T(8,128)(2,1)} %get-tuple-element.37), channel_id=1, source_target_pairs={{0,4},{2,6},{4,0},{6,2},{8,12},{10,14},{12,8},{14,10},{16,20},{18,... | collective-permute-start | bytes 3145736 | tf_op jit(solution)/shard_map/ppermute | solution.py:398
  170.6 46.9 %all-to-all-start.3 = ((bf16[16,128,256]{2,1,0:T(8,128)(2,1)}), bf16[16,128,256]{2,1,0:T(8,128)(2,1)S(1)}, u32[]{:S(2)}, u32[]{:S(2)}) async-start(bf16[16,128,256]{2,1,0:T(8,128)(2,1)} %add_convert_fusion), calls=%async_computation.3 | async-start | bytes 2097152 | tf_op jit(solution)/shard_map/all_to_all | solution.py:377
  175.3 38.2 %copy-start.3 = (bf16[256,1024]{1,0:T(8,128)(2,1)S(1)}, bf16[256,1024]{1,0:T(8,128)(2,1)}, u32[]{:S(2)}) copy-start(bf16[256,1024]{1,0:T(8,128)(2,1)} %get-tuple-element.31) | copy-start | bytes 1572868
  175.3 38.2 %copy-start.4 = (bf16[256,1024]{1,0:T(8,128)(2,1)S(1)}, bf16[256,1024]{1,0:T(8,128)(2,1)}, u32[]{:S(2)}) copy-start(bf16[256,1024]{1,0:T(8,128)(2,1)} %get-tuple-element.38) | copy-start | bytes 1572868
  175.3 38.2 %copy-start.5 = (bf16[256,1024]{1,0:T(8,128)(2,1)S(1)}, bf16[256,1024]{1,0:T(8,128)(2,1)}, u32[]{:S(2)}) copy-start(bf16[256,1024]{1,0:T(8,128)(2,1)} %get-tuple-element.35) | copy-start | bytes 1572868
  175.3 38.2 %copy-start.6 = (bf16[256,1024]{1,0:T(8,128)(2,1)S(1)}, bf16[256,1024]{1,0:T(8,128)(2,1)}, u32[]{:S(2)}) copy-start(bf16[256,1024]{1,0:T(8,128)(2,1)} %get-tuple-element.39) | copy-start | bytes 1572868
  216.6 6.4 %collective-permute-start.15 = (bf16[2,128,256]{2,1,0:T(8,128)(2,1)S(1)}, bf16[2,128,256]{2,1,0:T(8,128)(2,1)S(1)}, u32[]{:S(2)}, u32[]{:S(2)}) collective-permute-start(bf16[2,128,256]{2,1,0:T(8,128)(2,1)S(1)} %get-tuple-element.49), channel_id=1, source_target_pairs={{0,4},{2,6},{4,0},{6,2},{8,12},{10,14},{12,8},{14,10},{16,20},{18,... | collective-permute-start | bytes 393224 | tf_op jit(solution)/shard_map/ppermute | solution.py:404
  217.8 6.7 %collective-permute-start.16 = (bf16[2,128,256]{2,1,0:T(8,128)(2,1)S(1)}, bf16[2,128,256]{2,1,0:T(8,128)(2,1)S(1)}, u32[]{:S(2)}, u32[]{:S(2)}) collective-permute-start(bf16[2,128,256]{2,1,0:T(8,128)(2,1)S(1)} %get-tuple-element.51), channel_id=1, source_target_pairs={{0,4},{2,6},{4,0},{6,2},{8,12},{10,14},{12,8},{14,10},{16,20},{18,... | collective-permute-start | bytes 393224 | tf_op jit(solution)/shard_map/ppermute | solution.py:404
where the time goes:
time: 227 us; the launch traced here: 226 us
  waiting for transfers between devices  88.9 us (39%)
  Pallas kernels  64.2 us (28%)
  blocking collectives  30.1 us (13%)
  starting transfers between devices  29.5 us (13%)
  other arithmetic  8.76 us (4%)
  local copies, waits for them, and re-layouts  3.82 us (2%)
    pallas_call x2, Pallas kernels, quad_attention(): pl.pallas_call(functools.partial(quad_kernel, slots=slots, lines=lines, k...  52.9 us
    ppermute x2, waiting for transfers between devices, quad(): far_parts.append(lax.ppermute(far, 'seq', sideways))  36.8 us
    all_to_all x1, blocking collectives, along_line(): lax.all_to_all(array, 'seq', split_axis=0, concat_axis=0, tiled=True, axi...  30.1 us
    ppermute x3, waiting for transfers between devices, trade(): lax.ppermute(parts[2], ('seq', 'head'), corner)  22.7 us
    ppermute x3, waiting for transfers between devices, trade(): lax.ppermute(parts[0], 'head', across)  17.2 us
    all_to_all x3, starting transfers between devices, along_line(): lax.all_to_all(array, 'seq', split_axis=0, concat_axis=0, tiled=True, axi...  13.1 us
    ppermute x3, waiting for transfers between devices, trade(): lax.ppermute(parts[1], 'seq', sideways)  6.1 us
    ppermute x2, waiting for transfers between devices, quad(): grad_parts.append((summed[0], lax.ppermute(summed[1], 'seq', sideways)))  5.35 us
  transfers between devices with their start and end apart: 20, of which 14 were waited for; matrix products, arithmetic and copies ran while one was open for 4% of the time, Pallas kernels for 27%

commit v1 on v0

--- a/solution.py
+++ b/solution.py
@@ -14,7 +14,6 @@
 BLOCK_TOKENS = 128
 GROUP = QUERY_HEADS // KEY_VALUE_HEADS
 GROUP_WIDTH = GROUP * HEAD_SIZE
-HEADS_AT_ONCE = 4
 LOG2E = 1.4426950408889634
 FACTOR = HEAD_SIZE ** (-0.5)
 
@@ -26,6 +25,10 @@
 
 def dot(a, b, dims):
     return lax.dot_general(a, b, dims, preferred_element_type=jnp.float32)
+
+
+def held(*arrays):
+    return [pltpu.with_memory_space_constraint(array, pltpu.HBM) for array in arrays]
 
 
 def stored_index(block_position):
@@ -35,55 +38,47 @@
     return jnp.sum(jnp.where(matches, stored[None, :], 0), axis=1)
 
 
-def attend_block(i, slot_ref, q_ref, g_ref, kv_ref, a_ref, dq_ref, total, keys_at, values_at, part, slots):
+def attend_block(i, slot_ref, q_ref, g_ref, kv_ref, a_ref, dq_ref, total, keys_at, values_at, slots):
     b = BLOCK_TOKENS
     d = HEAD_SIZE
-    rows = HEADS_AT_ONCE * b
+    rows = GROUP * b
+    at = [jnp.maximum(slot_ref[i * slots + e], 0) for e in range(slots)]
+    bias = [jnp.where(slot_ref[i * slots + e] >= 0, 0.0, jnp.inf).astype(jnp.float32) for e in range(slots)]
     for e in range(slots):
-        at = jnp.maximum(slot_ref[i * slots + e], 0)
-        keys_at[e * b : (e + 1) * b, :] = kv_ref[at, :, :d]
-        values_at[e * b : (e + 1) * b, :] = kv_ref[at, :, d:]
-    bias = [
-        jnp.where(slot_ref[i * slots + e] >= 0, 0.0, jnp.inf).astype(jnp.float32) for e in range(slots)
-    ]
-    part[...] = jnp.zeros_like(part)
-
-    def heads(j, carry):
-        spans = [pl.ds((j * HEADS_AT_ONCE + t) * d, d) for t in range(HEADS_AT_ONCE)]
-        q = jnp.concatenate([q_ref[i, :, span] for span in spans], axis=0)
-        g = jnp.concatenate([g_ref[i, :, span] for span in spans], axis=0)
-        k = keys_at[...]
-        v = values_at[...]
-        s = dot(q, k, NT)
-        column = lax.broadcasted_iota(jnp.int32, (rows, b), 1)
-        row = lax.broadcasted_iota(jnp.int32, (rows, b), 0) & (b - 1)
-        tiles = [jnp.where(column <= row, s[:, :b], -jnp.inf)]
-        tiles += [s[:, e * b : (e + 1) * b] for e in range(1, slots)]
-        high = tiles[0]
-        for e in range(1, slots):
-            high = jnp.maximum(high, tiles[e] - bias[e])
-        high = jnp.max(high, axis=1, keepdims=True) * (FACTOR * LOG2E)
-        powers = [jnp.exp2(tiles[e] * (FACTOR * LOG2E) - (high + bias[e])) for e in range(slots)]
-        inverse = 1.0 / jnp.sum(functools.reduce(jnp.add, powers), axis=1, keepdims=True)
-        probs = jnp.concatenate([power * inverse for power in powers], axis=1)
-        probs_half = probs.astype(jnp.bfloat16)
-        out = dot(probs_half, v, NN).astype(jnp.bfloat16)
-        dprobs = dot(g, v, NT)
-        delta = jnp.sum(g.astype(jnp.float32) * out.astype(jnp.float32), axis=1, keepdims=True)
-        dscores = (probs * (dprobs - delta)).astype(jnp.bfloat16)
-        dq = (dot(dscores, k, NN) * FACTOR).astype(jnp.bfloat16)
-        part[:, :d] += dot(dscores, q, TN)
-        part[:, d:] += dot(probs_half, g, TN)
-        for t, span in enumerate(spans):
-            a_ref[i, :, span] = out[t * b : (t + 1) * b]
-            dq_ref[i, :, span] = dq[t * b : (t + 1) * b]
-        return carry
-
-    lax.fori_loop(0, GROUP // HEADS_AT_ONCE, heads, 0)
+        keys_at[e * b : (e + 1) * b, :] = kv_ref[at[e], :, :d]
+        values_at[e * b : (e + 1) * b, :] = kv_ref[at[e], :, d:]
+    spans = [slice(t * d, (t + 1) * d) for t in range(GROUP)]
+    q = jnp.concatenate([q_ref[i, :, span] for span in spans], axis=0)
+    g = jnp.concatenate([g_ref[i, :, span] for span in spans], axis=0)
+    k = keys_at[...]
+    v = values_at[...]
+    s = dot(q, k, NT)
+    column = lax.broadcasted_iota(jnp.int32, (rows, b), 1)
+    row = lax.broadcasted_iota(jnp.int32, (rows, b), 0) & (b - 1)
+    tiles = [jnp.where(column <= row, s[:, :b], -jnp.inf)]
+    tiles += [s[:, e * b : (e + 1) * b] for e in range(1, slots)]
+    high = tiles[0]
+    for e in range(1, slots):
+        high = jnp.maximum(high, tiles[e] - bias[e])
+    high = jnp.max(high, axis=1, keepdims=True) * (FACTOR * LOG2E)
+    powers = [jnp.exp2(tiles[e] * (FACTOR * LOG2E) - (high + bias[e])) for e in range(slots)]
+    inverse = 1.0 / jnp.sum(functools.reduce(jnp.add, powers), axis=1, keepdims=True)
+    probs = jnp.concatenate([power * inverse for power in powers], axis=1)
+    probs_half = probs.astype(jnp.bfloat16)
+    out = dot(probs_half, v, NN).astype(jnp.bfloat16)
+    dprobs = dot(g, v, NT)
+    delta = jnp.sum(g.astype(jnp.float32) * out.astype(jnp.float32), axis=1, keepdims=True)
+    dscores = (probs * (dprobs - delta)).astype(jnp.bfloat16)
+    dq = (dot(dscores, k, NN) * FACTOR).astype(jnp.bfloat16)
+    for t, span in enumerate(spans):
+        a_ref[i, :, span] = out[t * b : (t + 1) * b]
+        dq_ref[i, :, span] = dq[t * b : (t + 1) * b]
+    dk = dot(q, dscores, TN) * FACTOR
+    dv = dot(g, probs_half, TN)
     for e in range(slots):
-        at = jnp.maximum(slot_ref[i * slots + e], 0)
-        total[at, :, :d] += part[e * b : (e + 1) * b, :d] * FACTOR
-        total[at, :, d:] += part[e * b : (e + 1) * b, d:]
+        span = slice(e * b, (e + 1) * b)
+        total[at[e], :, :d] += jnp.transpose(dk[:, span])
+        total[at[e], :, d:] += jnp.transpose(dv[:, span])
 
 
 def cost(blocks, slots, stored, wide):
@@ -99,15 +94,14 @@
     return [
         pltpu.VMEM((slots * BLOCK_TOKENS, HEAD_SIZE), jnp.bfloat16),
         pltpu.VMEM((slots * BLOCK_TOKENS, HEAD_SIZE), jnp.bfloat16),
-        pltpu.VMEM((slots * BLOCK_TOKENS, 2 * HEAD_SIZE), jnp.float32),
     ]
 
 
-def plain_kernel(slot_ref, q_ref, g_ref, kv_ref, a_ref, dq_ref, total, keys_at, values_at, part, *, slots):
+def plain_kernel(slot_ref, q_ref, g_ref, kv_ref, a_ref, dq_ref, total, keys_at, values_at, *, slots):
     total[...] = jnp.zeros_like(total)
 
     def block(i, carry):
-        attend_block(i, slot_ref, q_ref, g_ref, kv_ref, a_ref, dq_ref, total, keys_at, values_at, part, slots)
+        attend_block(i, slot_ref, q_ref, g_ref, kv_ref, a_ref, dq_ref, total, keys_at, values_at, slots)
         return carry
 
     lax.fori_loop(0, q_ref.shape[0], block, 0)
@@ -174,7 +168,7 @@
 def quad_kernel(listed_ref, position_ref, q_ref, g_ref, *refs, slots, lines, kv_heads, head):
     pieces, refs = refs[:3], refs[3:]
     kv_line, kv_beside, a_own, dq_own, far, total_line, total_beside = refs[:7]
-    located, slot, q_at, g_at, kv_at, a_at, dq_at, total, keys_at, values_at, part, kv_sem, in_sem, out_sem = refs[7:]
+    located, slot, q_at, g_at, kv_at, a_at, dq_at, total, keys_at, values_at, kv_sem, in_sem, out_sem = refs[7:]
     s = lax.axis_index("seq")
     h = lax.axis_index("head")
     x = (s >> 1) & 1
@@ -201,7 +195,7 @@
     def entry(n, carry):
         i, e = n // slots, n % slots
         stored = ((s ^ (2 * (i >> 1))) * 2) + (h ^ (i & 1))
-        b = listed_ref[position_ref[stored], e]
+        b = listed_ref[e, position_ref[stored]]
         home = located[jnp.maximum(b, 0)]
         seq_home = home >> 1
         where_ = ((seq_home ^ s) & 1) * half + (seq_home >> 2) * 4
@@ -211,11 +205,13 @@
 
     lax.fori_loop(0, 4 * slots, entry, 0)
     total[...] = jnp.zeros_like(total)
-    for fetch in fetches:
+    for fetch in fetches[:2]:
         fetch.wait()
 
     def block(i, carry):
-        attend_block(i, slot, q_at, g_at, kv_at, a_at, dq_at, total, keys_at, values_at, part, slots)
+        pltpu.make_async_copy(q_at.at[i], q_at.at[i], in_sem.at[0, i]).wait()
+        pltpu.make_async_copy(g_at.at[i], g_at.at[i], in_sem.at[1, i]).wait()
+        attend_block(i, slot, q_at, g_at, kv_at, a_at, dq_at, total, keys_at, values_at, slots)
         row = pl.ds(pl.multiple_of((h ^ (i & 1)) * BLOCK_TOKENS, BLOCK_TOKENS), BLOCK_TOKENS)
 
         @pl.when(i < 2)
@@ -238,12 +234,12 @@
 
 
 def quad_attention(kv_blocks, block_position, queries, output_gradient, pieces, kv_line, kv_beside, lines, kv_heads, head):
-    outside = pl.BlockSpec(memory_space=pltpu.HBM)
+    outside = pl.BlockSpec(memory_space=pl.ANY)
     inside = pl.BlockSpec(memory_space=pltpu.VMEM)
     slots = kv_blocks.shape[1]
     half = lines * 4
-    own = jax.ShapeDtypeStruct((2 * BLOCK_TOKENS, GROUP_WIDTH), jnp.bfloat16)
-    sums = jax.ShapeDtypeStruct((half, BLOCK_TOKENS, 2 * HEAD_SIZE), jnp.bfloat16)
+    own = pltpu.HBM((2 * BLOCK_TOKENS, GROUP_WIDTH), jnp.bfloat16)
+    sums = pltpu.HBM((half, BLOCK_TOKENS, 2 * HEAD_SIZE), jnp.bfloat16)
     wide = pltpu.VMEM((4, BLOCK_TOKENS, GROUP_WIDTH), jnp.bfloat16)
     return pl.pallas_call(
         functools.partial(quad_kernel, slots=slots, lines=lines, kv_heads=kv_heads, head=head),
@@ -267,10 +263,10 @@
                 pltpu.SemaphoreType.DMA((3,)),
             ],
         ),
-        out_shape=[own, own, jax.ShapeDtypeStruct((2, *own.shape), jnp.bfloat16), sums, sums],
-        compiler_params=pltpu.CompilerParams(vmem_limit_bytes=60 << 20),
+        out_shape=[own, own, pltpu.HBM((2, 2 * BLOCK_TOKENS, GROUP_WIDTH), jnp.bfloat16), sums, sums],
+        compiler_params=pltpu.CompilerParams(vmem_limit_bytes=44 << 20),
         cost_estimate=cost(4, slots, 2 * half, 2),
-    )(kv_blocks, block_position, queries, output_gradient, *pieces, kv_line, kv_beside)
+    )(jnp.transpose(kv_blocks), block_position, *held(queries, output_gradient), *pieces, kv_line, kv_beside)
 
 
 def pack_kernel(keys_ref, values_ref, *outs, kv_heads):
@@ -287,13 +283,13 @@
 
 def pack(keys, values, kv_heads):
     inside = pl.BlockSpec(memory_space=pltpu.VMEM)
-    shape = jax.ShapeDtypeStruct((kv_heads, BLOCK_TOKENS, 2 * HEAD_SIZE), jnp.bfloat16)
+    shape = pltpu.HBM((kv_heads, BLOCK_TOKENS, 2 * HEAD_SIZE), jnp.bfloat16)
     return pl.pallas_call(
         functools.partial(pack_kernel, kv_heads=kv_heads),
         in_specs=[inside] * 2,
         out_specs=[inside] * 4,
         out_shape=[shape] * 4,
-    )(keys, values)
+    )(*held(keys, values))
 
 
 def pack_wide_kernel(q_ref, g_ref, *refs, kv_heads, head):
@@ -321,36 +317,88 @@
 
 def pack_wide(queries, output_gradient, kv_heads, head):
     outside = pl.BlockSpec(memory_space=pltpu.HBM)
-    shape = jax.ShapeDtypeStruct((2, BLOCK_TOKENS, GROUP_WIDTH), jnp.bfloat16)
+    shape = pltpu.HBM((2, BLOCK_TOKENS, GROUP_WIDTH), jnp.bfloat16)
     return pl.pallas_call(
         functools.partial(pack_wide_kernel, kv_heads=kv_heads, head=head),
         in_specs=[outside] * 2,
         out_specs=[outside] * 3,
         out_shape=[shape] * 3,
         scratch_shapes=[
-            pltpu.VMEM((3, *shape.shape), jnp.bfloat16),
+            pltpu.VMEM((3, 2, BLOCK_TOKENS, GROUP_WIDTH), jnp.bfloat16),
             pltpu.SemaphoreType.DMA((3, 2)),
             pltpu.SemaphoreType.DMA((3,)),
         ],
         cost_estimate=pl.CostEstimate(flops=0, transcendentals=0, bytes_accessed=12 * BLOCK_TOKENS * GROUP_WIDTH * 2),
-    )(queries, output_gradient)
+    )(*held(queries, output_gradient))
 
 
 def spread_kernel(*refs, head):
-    out = refs[-1]
-    for line in range(out.shape[0] // 4):
-        for n in range(4):
-            out[line * 4 + n] = refs[n][head]
+    parts, (out, at, in_sem, out_sem) = refs[:4], refs[4:]
+    fetches = [pltpu.make_async_copy(part.at[head], at.at[n], in_sem.at[n]) for n, part in enumerate(parts)]
+    for fetch in fetches:
+        fetch.start()
+    for fetch in fetches:
+        fetch.wait()
+    stores = [
+        pltpu.make_async_copy(at, out.at[pl.ds(line * 4, 4)], out_sem.at[line]) for line in range(out.shape[0] // 4)
+    ]
+    for store in stores:
+        store.start()
+    for store in stores:
+        store.wait()
 
 
 def spread(parts, head, lines):
-    inside = pl.BlockSpec(memory_space=pltpu.VMEM)
+    anywhere = pl.BlockSpec(memory_space=pl.ANY)
     return pl.pallas_call(
         functools.partial(spread_kernel, head=head),
-        in_specs=[inside] * 4,
-        out_specs=inside,
-        out_shape=jax.ShapeDtypeStruct((lines * 4, BLOCK_TOKENS, 2 * HEAD_SIZE), jnp.bfloat16),
+        in_specs=[anywhere] * 4,
+        out_specs=anywhere,
+        out_shape=pltpu.HBM((lines * 4, BLOCK_TOKENS, 2 * HEAD_SIZE), jnp.bfloat16),
+        scratch_shapes=[
+            pltpu.VMEM((4, BLOCK_TOKENS, 2 * HEAD_SIZE), jnp.bfloat16),
+            pltpu.SemaphoreType.DMA((4,)),
+            pltpu.SemaphoreType.DMA((lines,)),
+        ],
+        compiler_params=pltpu.CompilerParams(vmem_limit_bytes=8 << 20),
     )(*parts)
+
+
+def merge_kernel(a_ref, b_ref, out_ref, at, out_at, in_sem, out_sem, *, lines):
+    fetches = [
+        [pltpu.make_async_copy(ref.at[pl.ds(n * 4, 4)], at.at[m, n], in_sem.at[m, n]) for m, ref in enumerate((a_ref, b_ref))]
+        for n in range(lines)
+    ]
+    for pair in fetches:
+        for fetch in pair:
+            fetch.start()
+    stores = []
+    for n in range(lines):
+        for fetch in fetches[n]:
+            fetch.wait()
+        out_at[n] = (at[0, n].astype(jnp.float32) + at[1, n].astype(jnp.float32)).astype(jnp.bfloat16)
+        stores.append(pltpu.make_async_copy(out_at.at[n], out_ref.at[pl.ds(n * 4, 4)], out_sem.at[n]))
+        stores[n].start()
+    for store in stores:
+        store.wait()
+
+
+def merge(a, b, lines):
+    anywhere = pl.BlockSpec(memory_space=pl.ANY)
+    piece = (4, *a.shape[1:])
+    return pl.pallas_call(
+        functools.partial(merge_kernel, lines=lines),
+        in_specs=[anywhere] * 2,
+        out_specs=anywhere,
+        out_shape=pltpu.HBM(a.shape, jnp.bfloat16),
+        scratch_shapes=[
+            pltpu.VMEM((2, lines, *piece), jnp.bfloat16),
+            pltpu.VMEM((lines, *piece), jnp.bfloat16),
+            pltpu.SemaphoreType.DMA((2, lines)),
+            pltpu.SemaphoreType.DMA((lines,)),
+        ],
+        compiler_params=pltpu.CompilerParams(vmem_limit_bytes=16 << 20),
+    )(a, b)
 
 
 def quad(queries, keys, values, output_gradient, kv_blocks, block_position):
@@ -397,8 +445,8 @@
         arrived = lax.ppermute(total_beside, "seq", beside)
         far_parts.append(lax.ppermute(far, "seq", sideways))
         own_parts.append((a_own, dq_own))
-        total = total_line.astype(jnp.float32) + arrived.astype(jnp.float32)
-        returned = along_line(total.astype(jnp.bfloat16))
+        total = merge(total_line, arrived, lines)
+        returned = along_line(total)
         returned = returned.reshape(lines, 2, 2, BLOCK_TOKENS, 2 * HEAD_SIZE)
         summed = jnp.sum(returned.astype(jnp.float32), axis=0).astype(jnp.bfloat16)
         grad_parts.append((summed[0], lax.ppermute(summed[1], "seq", sideways)))

time: 227 us -> 213 us (0.938)
  Pallas kernels: 64.2 us -> 53.6 us
  other arithmetic: 8.76 us -> 4.94 us
    pallas_call x2, Pallas kernels: 52.9 us -> 41.9 us  [quad_attention(): pl.pallas_call(functools.partial(quad_kernel, slots=slots, lines=lines, k...]
    convert_element_type x2 -> x0, other arithmetic: 3.82 us -> none  [quad(): returned = along_line(total.astype(jnp.bfloat16))]
    pallas_call x2 -> x4, Pallas kernels: 4.64 us -> 5.28 us  [the longest x2 2.69 us: spread(): pl.pallas_call(functools.partial(spread_kernel, head=head), in_specs=[any...]
  transfers between devices with their start and end apart: 20 -> 20, of which waited for: 14 -> 14; matrix products, arithmetic and copies ran while one was open for 4% -> 2% of each run, Pallas kernels for 27% -> 24%
where the time goes in v1:
time: 213 us; the launch traced here: 212 us
  waiting for transfers between devices  89.6 us (42%)
  Pallas kernels  53.6 us (25%)
  blocking collectives  30.1 us (14%)
  starting transfers between devices  29.6 us (14%)
  other arithmetic  4.94 us (2%)
  local copies, waits for them, and re-layouts  3.63 us (2%)
    pallas_call x2, Pallas kernels, quad_attention(): pl.pallas_call(functools.partial(quad_kernel, slots=slots, lines=lines, k...  41.9 us
    ppermute x2, waiting for transfers between devices, quad(): far_parts.append(lax.ppermute(far, 'seq', sideways))  36.8 us
    all_to_all x1, blocking collectives, along_line(): lax.all_to_all(array, 'seq', split_axis=0, concat_axis=0, tiled=True, axi...  30.1 us
    ppermute x3, waiting for transfers between devices, trade(): lax.ppermute(parts[2], ('seq', 'head'), corner)  22.9 us
    ppermute x3, waiting for transfers between devices, trade(): lax.ppermute(parts[0], 'head', across)  17.9 us
    all_to_all x3, starting transfers between devices, along_line(): lax.all_to_all(array, 'seq', split_axis=0, concat_axis=0, tiled=True, axi...  13.1 us
    ppermute x3, waiting for transfers between devices, trade(): lax.ppermute(parts[1], 'seq', sideways)  5.93 us
    ppermute x2, waiting for transfers between devices, quad(): grad_parts.append((summed[0], lax.ppermute(summed[1], 'seq', sideways)))  5.35 us
  transfers between devices with their start and end apart: 20, of which 14 were waited for; matrix products, arithmetic and copies ran while one was open for 2% of the time, Pallas kernels for 24%

profile of v1, /device:TPU:0, one launch (start us, length us, event | category | flops | bytes accessed | tf_op | source)
XLA Modules:
  0.0 212.3 jit_solution(15428708464968800381)
XLA Ops:
  0.6 1.9 shard_map.94
  2.6 3.0 %collective-permute-start.3 = (bf16[2,128,256]{2,1,0:T(8,128)(2,1)}, bf16[2,128,256]{2,1,0:T(8,128)(2,1)S(1)}, u32[]{:S(2)}, u32[]{:S(2)}) collective-permute-start(bf16[2,128,256]{2,1,0:T(8,128)(2,1)} %get-tuple-element.28), channel_id=1, source_target_pairs={{0,1},{1,0},{2,3},{3,2},{4,5},{5,4},{6,7},{7,6},{8,9},{9,8},{10,11... | collective-permute-start | bytes 393224 | tf_op jit(solution)/shard_map/ppermute | solution.py:419
  5.6 1.5 collective-permute-start.4
  7.1 0.0 collective-permute-start.5
  7.1 2.2 %collective-permute-done.3.refs_1_ = bf16[2,128,256]{2,1,0:T(8,128)(2,1)S(1)} collective-permute-done((bf16[2,128,256]{2,1,0:T(8,128)(2,1)}, bf16[2,128,256]{2,1,0:T(8,128)(2,1)S(1)}, u32[]{:S(2)}, u32[]{:S(2)}) %collective-permute-start.3) | collective-permute-done | bytes 131104 | tf_op jit(solution)/shard_map/ppermute | solution.py:419
  9.3 2.9 %collective-permute-done.4.refs_2_ = bf16[2,128,256]{2,1,0:T(8,128)(2,1)S(1)} collective-permute-done((bf16[2,128,256]{2,1,0:T(8,128)(2,1)}, bf16[2,128,256]{2,1,0:T(8,128)(2,1)S(1)}, u32[]{:S(2)}, u32[]{:S(2)}) %collective-permute-start.4) | collective-permute-done | bytes 131104 | tf_op jit(solution)/shard_map/ppermute | solution.py:420
  12.1 1.1 collective-permute-done.5.refs_3_
  13.3 0.9 copy-done.2
  14.2 1.3 shard_map.95
  15.5 30.1 %all_to_all.20.refs_3_ = bf16[16,128,256]{2,1,0:T(8,128)(2,1)S(1)} all-to-all(bf16[16,128,256]{2,1,0:T(8,128)(2,1)} %shard_map.95), channel_id=1, replica_groups={{0,8,16,24},{2,10,18,26},{4,12,20,28},{6,14,22,30},{1,9,17,25},{3,11,19..., dimensions={0} | all-to-all | bytes 2097152 | tf_op jit(solution)/shard_map/all_to_all | solution.py:425
  45.6 0.0 collective-permute-start.6
  45.6 1.4 shard_map.98
  47.0 3.5 %all-to-all-start.1 = ((bf16[16,128,256]{2,1,0:T(8,128)(2,1)}), bf16[16,128,256]{2,1,0:T(8,128)(2,1)S(1)}, u32[]{:S(2)}, u32[]{:S(2)}) async-start(bf16[16,128,256]{2,1,0:T(8,128)(2,1)} %shard_map.98), calls=%async_computation.1 | async-start | bytes 2097152 | tf_op jit(solution)/shard_map/all_to_all | solution.py:425
  50.5 0.0 copy-start.3
  50.5 0.0 copy-start.4
  50.5 2.3 %shard_map.93 = (bf16[2,128,1024]{2,1,0:T(8,128)(2,1)}, bf16[2,128,1024]{2,1,0:T(8,128)(2,1)}, bf16[2,128,1024]{2,1,0:T(8,128)(2,1)}) custom-call(bf16[1,128,8192]{2,1,0:T(8,128)(2,1)} %q_ref.7, bf16[1,128,8192]{2,1,0:T(8,128)(2,1)} %g_ref.7), custom_call_target="tpu_custom_call" | custom-call | bytes 3145728 | tf_op jit(solution)/shard_map/pallas_call | solution.py:321
  52.8 0.9 collective-permute-start
  53.7 1.5 collective-permute-start.1
  55.2 1.1 collective-permute-start.2
  56.4 11.0 %collective-permute-done.refs_0_ = bf16[2,128,1024]{2,1,0:T(8,128)(2,1)S(1)} collective-permute-done((bf16[2,128,1024]{2,1,0:T(8,128)(2,1)}, bf16[2,128,1024]{2,1,0:T(8,128)(2,1)S(1)}, u32[]{:S(2)}, u32[]{:S(2)}) %collective-permute-start) | collective-permute-done | bytes 524320 | tf_op jit(solution)/shard_map/ppermute | solution.py:419
  67.4 1.3 collective-permute-done.1.refs_1_
  68.7 11.1 %collective-permute-done.2.refs_2_ = bf16[2,128,1024]{2,1,0:T(8,128)(2,1)S(1)} collective-permute-done((bf16[2,128,1024]{2,1,0:T(8,128)(2,1)}, bf16[2,128,1024]{2,1,0:T(8,128)(2,1)S(1)}, u32[]{:S(2)}, u32[]{:S(2)}) %collective-permute-start.2) | collective-permute-done | bytes 524320 | tf_op jit(solution)/shard_map/ppermute | solution.py:421
  79.8 0.0 collective-permute-done.6.refs_4_
  79.8 0.0 copy-done.3
  79.8 20.9 %shard_map.96 = (bf16[256,1024]{1,0:T(8,128)(2,1)}, bf16[256,1024]{1,0:T(8,128)(2,1)}, bf16[2,256,1024]{2,1,0:T(8,128)(2,1)}, bf16[16,128,256]{2,1,0:T(8,128)(2,1)}, bf16[16,128,256]{2,1,0:T(8,128)(2,1)}) custom-call(s32[8,32]{1,0:T(8,128)S(1)} %bitcast.17, s32[32]{0:T(128)S(1)} %copy-done.4, bf16[1,128,8192]{2,1,0:T(8,128)(2,1)} %q_ref.7, ...), custom_call_target="tpu_custom_call" | custom-call | flops 5368709120 | bytes 8388608 | tf_op jit(solution)/shard_map/pallas_call | solution.py:244
  100.7 0.0 copy-start.1
  100.7 0.1 collective-permute-start.13
  100.8 0.0 all-to-all-done.1.refs_3_
  100.8 0.5 collective-permute-start.10
  101.3 2.3 %shard_map.97 = (bf16[2,128,1024]{2,1,0:T(8,128)(2,1)}, bf16[2,128,1024]{2,1,0:T(8,128)(2,1)}, bf16[2,128,1024]{2,1,0:T(8,128)(2,1)}) custom-call(bf16[1,128,8192]{2,1,0:T(8,128)(2,1)} %q_ref.7, bf16[1,128,8192]{2,1,0:T(8,128)(2,1)} %g_ref.7), custom_call_target="tpu_custom_call" | custom-call | bytes 3145728 | tf_op jit(solution)/shard_map/pallas_call | solution.py:321
  103.6 0.9 collective-permute-start.7
  104.5 1.5 collective-permute-start.8
  106.0 1.1 collective-permute-start.9
  107.2 0.0 collective-permute-done.13.b_ref
  107.2 1.3 shard_map.100
  108.5 4.8 %all-to-all-start.2 = ((bf16[16,128,256]{2,1,0:T(8,128)(2,1)}), bf16[16,128,256]{2,1,0:T(8,128)(2,1)S(1)}, u32[]{:S(2)}, u32[]{:S(2)}) async-start(bf16[16,128,256]{2,1,0:T(8,128)(2,1)} %shard_map.100), calls=%async_computation.2 | async-start | bytes 2097152 | tf_op jit(solution)/shard_map/all_to_all | solution.py:425
  113.2 4.6 %collective-permute-done.7.refs_0_ = bf16[2,128,1024]{2,1,0:T(8,128)(2,1)} collective-permute-done((bf16[2,128,1024]{2,1,0:T(8,128)(2,1)}, bf16[2,128,1024]{2,1,0:T(8,128)(2,1)}, u32[]{:S(2)}, u32[]{:S(2)}) %collective-permute-start.7) | collective-permute-done | bytes 524320 | tf_op jit(solution)/shard_map/ppermute | solution.py:419
  117.9 1.7 collective-permute-done.8.refs_1_
  119.6 10.7 %collective-permute-done.9.refs_2_ = bf16[2,128,1024]{2,1,0:T(8,128)(2,1)} collective-permute-done((bf16[2,128,1024]{2,1,0:T(8,128)(2,1)}, bf16[2,128,1024]{2,1,0:T(8,128)(2,1)}, u32[]{:S(2)}, u32[]{:S(2)}) %collective-permute-start.9) | collective-permute-done | bytes 524320 | tf_op jit(solution)/shard_map/ppermute | solution.py:421
  130.3 0.0 collective-permute-done.10.refs_4_
  130.3 21.0 %shard_map.99 = (bf16[256,1024]{1,0:T(8,128)(2,1)}, bf16[256,1024]{1,0:T(8,128)(2,1)}, bf16[2,256,1024]{2,1,0:T(8,128)(2,1)}, bf16[16,128,256]{2,1,0:T(8,128)(2,1)}, bf16[16,128,256]{2,1,0:T(8,128)(2,1)}) custom-call(s32[8,32]{1,0:T(8,128)S(1)} %bitcast.18, s32[32]{0:T(128)S(1)} %copy-done.4, bf16[1,128,8192]{2,1,0:T(8,128)(2,1)} %q_ref.7, ...), custom_call_target="tpu_custom_call" | custom-call | flops 5368709120 | bytes 8388608 | tf_op jit(solution)/shard_map/pallas_call | solution.py:244
  151.3 0.1 collective-permute-start.14
  151.4 0.9 collective-permute-start.11
  152.2 1.2 collective-permute-start.12
  153.5 0.8 collective-permute-done.14.b_ref
  154.2 1.2 copy-done
  155.5 1.3 shard_map.101
  156.7 0.0 all-to-all-done.2
  156.8 4.8 %all-to-all-start.3 = ((bf16[16,128,256]{2,1,0:T(8,128)(2,1)}), bf16[16,128,256]{2,1,0:T(8,128)(2,1)S(1)}, u32[]{:S(2)}, u32[]{:S(2)}) async-start(bf16[16,128,256]{2,1,0:T(8,128)(2,1)} %shard_map.101), calls=%async_computation.3 | async-start | bytes 2097152 | tf_op jit(solution)/shard_map/all_to_all | solution.py:425
  161.5 16.2 %collective-permute-done.11 = bf16[2,256,1024]{2,1,0:T(8,128)(2,1)} collective-permute-done((bf16[2,256,1024]{2,1,0:T(8,128)(2,1)}, bf16[2,256,1024]{2,1,0:T(8,128)(2,1)}, u32[]{:S(2)}, u32[]{:S(2)}) %collective-permute-start.11) | collective-permute-done | bytes 1048608 | tf_op jit(solution)/shard_map/ppermute | solution.py:446
  177.8 1.3 fusion
  179.1 20.6 %collective-permute-done.12 = bf16[2,256,1024]{2,1,0:T(8,128)(2,1)S(1)} collective-permute-done((bf16[2,256,1024]{2,1,0:T(8,128)(2,1)}, bf16[2,256,1024]{2,1,0:T(8,128)(2,1)S(1)}, u32[]{:S(2)}, u32[]{:S(2)}) %collective-permute-start.12) | collective-permute-done | bytes 1048608 | tf_op jit(solution)/shard_map/ppermute | solution.py:446
  199.6 0.1 fusion.1
  199.7 2.8 %maximum_select_fusion = (bf16[1,256,4096]{2,1,0:T(8,128)(2,1)}, bf16[1,256,4096]{2,1,0:T(8,128)(2,1)}) fusion(bf16[1,256,1024]{2,1,0:T(8,128)(2,1)S(1)} %get-tuple-element.47, bf16[1,256,1024]{2,1,0:T(8,128)(2,1)S(1)} %get-tuple-element.45, bf16[1,256,1024]{2,1,0:T(8,128)(2,1)S(1)} %bitcast.23, bf16[1,256,1024]{2,1,0:T(8,128)(2,1)S(1)} %bitcast.21, ...), kind=kLoop, calls=%fused_computation | loop fusion | flops 35651584 | bytes 8388609 | tf_op jit(solution)/shard_map/jit(_where)/select_n | solution.py:455
  202.5 0.2 reduce_sum.24
  202.8 0.9 collective-permute-start.15
  203.7 0.0 all-to-all-done.3
  203.7 0.2 reduce_sum.25
  203.9 1.3 collective-permute-start.16
  205.2 4.0 %collective-permute-done.15 = bf16[2,128,256]{2,1,0:T(8,128)(2,1)S(1)} collective-permute-done((bf16[2,128,256]{2,1,0:T(8,128)(2,1)S(1)}, bf16[2,128,256]{2,1,0:T(8,128)(2,1)S(1)}, u32[]{:S(2)}, u32[]{:S(2)}) %collective-permute-start.15) | collective-permute-done | bytes 131104 | tf_op jit(solution)/shard_map/ppermute | solution.py:452
  209.2 1.4 collective-permute-done.16
  210.6 0.2 maximum_select_fusion.2
  210.8 0.8 reverse_select_fusion
  211.6 0.7 reverse_select_fusion.1
  (18 shorter events, 0.2 us)
Async XLA Ops:
  2.6 6.7 %collective-permute-start.3 = (bf16[2,128,256]{2,1,0:T(8,128)(2,1)}, bf16[2,128,256]{2,1,0:T(8,128)(2,1)S(1)}, u32[]{:S(2)}, u32[]{:S(2)}) collective-permute-start(bf16[2,128,256]{2,1,0:T(8,128)(2,1)} %get-tuple-element.28), channel_id=1, source_target_pairs={{0,1},{1,0},{2,3},{3,2},{4,5},{5,4},{6,7},{7,6},{8,9},{9,8},{10,11... | collective-permute-start | bytes 393224 | tf_op jit(solution)/shard_map/ppermute | solution.py:419
  5.6 6.6 %collective-permute-start.4 = (bf16[2,128,256]{2,1,0:T(8,128)(2,1)}, bf16[2,128,256]{2,1,0:T(8,128)(2,1)S(1)}, u32[]{:S(2)}, u32[]{:S(2)}) collective-permute-start(bf16[2,128,256]{2,1,0:T(8,128)(2,1)} %get-tuple-element.29), channel_id=1, source_target_pairs={{0,4},{2,6},{4,0},{6,2},{8,12},{10,14},{12,8},{14,10},{16,20},{18,... | collective-permute-start | bytes 393224 | tf_op jit(solution)/shard_map/ppermute | solution.py:420
  7.1 6.2 %collective-permute-start.5 = (bf16[2,128,256]{2,1,0:T(8,128)(2,1)}, bf16[2,128,256]{2,1,0:T(8,128)(2,1)S(1)}, u32[]{:S(2)}, u32[]{:S(2)}) collective-permute-start(bf16[2,128,256]{2,1,0:T(8,128)(2,1)} %get-tuple-element.30), channel_id=1, source_target_pairs={{0,5},{1,4},{2,7},{3,6},{4,1},{5,0},{6,3},{7,2},{8,13},{9,12},{10,... | collective-permute-start | bytes 393224 | tf_op jit(solution)/shard_map/ppermute | solution.py:421
  13.3 0.9 copy-start.2
  45.6 34.2 %collective-permute-start.6 = (bf16[16,128,256]{2,1,0:T(8,128)(2,1)S(1)}, bf16[16,128,256]{2,1,0:T(8,128)(2,1)S(1)}, u32[]{:S(2)}, u32[]{:S(2)}) collective-permute-start(bf16[16,128,256]{2,1,0:T(8,128)(2,1)S(1)} %all_to_all.20.refs_3_), channel_id=1, source_target_pairs={{0,2},{2,0},{4,6},{6,4},{8,10},{10,8},{12,14},{14,12},{16,18},{18,... | collective-permute-start | bytes 3145736 | tf_op jit(solution)/shard_map/ppermute | solution.py:441
  47.0 53.9 %all-to-all-start.1 = ((bf16[16,128,256]{2,1,0:T(8,128)(2,1)}), bf16[16,128,256]{2,1,0:T(8,128)(2,1)S(1)}, u32[]{:S(2)}, u32[]{:S(2)}) async-start(bf16[16,128,256]{2,1,0:T(8,128)(2,1)} %shard_map.98), calls=%async_computation.1 | async-start | bytes 2097152 | tf_op jit(solution)/shard_map/all_to_all | solution.py:425
  50.5 29.3 %copy-start.3 = (s32[32,8]{0,1:T(8,128)S(1)}, s32[32,8]{0,1:T(8,128)}, u32[]{:S(2)}) copy-start(s32[32,8]{0,1:T(8,128)} %param.10) | copy-start | bytes 3076
  50.5 29.3 %copy-start.4 = (s32[32]{0:T(128)S(1)}, s32[32]{0:T(128)}, u32[]{:S(2)}) copy-start(s32[32]{0:T(128)} %position_ref.3) | copy-start | bytes 388
  52.8 14.6 %collective-permute-start = (bf16[2,128,1024]{2,1,0:T(8,128)(2,1)}, bf16[2,128,1024]{2,1,0:T(8,128)(2,1)S(1)}, u32[]{:S(2)}, u32[]{:S(2)}) collective-permute-start(bf16[2,128,1024]{2,1,0:T(8,128)(2,1)} %get-tuple-element.24), channel_id=1, source_target_pairs={{0,1},{1,0},{2,3},{3,2},{4,5},{5,4},{6,7},{7,6},{8,9},{9,8},{10,11... | collective-permute-start | bytes 1572872 | tf_op jit(solution)/shard_map/ppermute | solution.py:419
  53.7 15.0 %collective-permute-start.1 = (bf16[2,128,1024]{2,1,0:T(8,128)(2,1)}, bf16[2,128,1024]{2,1,0:T(8,128)(2,1)S(1)}, u32[]{:S(2)}, u32[]{:S(2)}) collective-permute-start(bf16[2,128,1024]{2,1,0:T(8,128)(2,1)} %get-tuple-element.25), channel_id=1, source_target_pairs={{0,4},{2,6},{4,0},{6,2},{8,12},{10,14},{12,8},{14,10},{16,20},{18,... | collective-permute-start | bytes 1572872 | tf_op jit(solution)/shard_map/ppermute | solution.py:420
  55.2 24.6 %collective-permute-start.2 = (bf16[2,128,1024]{2,1,0:T(8,128)(2,1)}, bf16[2,128,1024]{2,1,0:T(8,128)(2,1)S(1)}, u32[]{:S(2)}, u32[]{:S(2)}) collective-permute-start(bf16[2,128,1024]{2,1,0:T(8,128)(2,1)} %get-tuple-element.26), channel_id=1, source_target_pairs={{0,5},{1,4},{2,7},{3,6},{4,1},{5,0},{6,3},{7,2},{8,13},{9,12},{10,... | collective-permute-start | bytes 1572872 | tf_op jit(solution)/shard_map/ppermute | solution.py:421
  100.7 6.4 %copy-start.1 = (bf16[16,128,256]{2,1,0:T(8,128)(2,1)S(1)}, bf16[16,128,256]{2,1,0:T(8,128)(2,1)}, u32[]{:S(2)}) copy-start(bf16[16,128,256]{2,1,0:T(8,128)(2,1)} %get-tuple-element.40.a_ref) | copy-start | bytes 3145732
  100.7 6.4 %collective-permute-start.13 = (bf16[16,128,256]{2,1,0:T(8,128)(2,1)}, bf16[16,128,256]{2,1,0:T(8,128)(2,1)S(1)}, u32[]{:S(2)}, u32[]{:S(2)}) collective-permute-start(bf16[16,128,256]{2,1,0:T(8,128)(2,1)} %get-tuple-element.41), channel_id=1, source_target_pairs={{0,2},{2,0},{4,6},{6,4},{8,10},{10,8},{12,14},{14,12},{16,18},{18,... | collective-permute-start | bytes 3145736 | tf_op jit(solution)/shard_map/ppermute | solution.py:445
  100.8 29.5 %collective-permute-start.10 = (bf16[16,128,256]{2,1,0:T(8,128)(2,1)S(1)}, bf16[16,128,256]{2,1,0:T(8,128)(2,1)}, u32[]{:S(2)}, u32[]{:S(2)}) collective-permute-start(bf16[16,128,256]{2,1,0:T(8,128)(2,1)S(1)} %all-to-all-done.1.refs_3_), channel_id=1, source_target_pairs={{0,2},{2,0},{4,6},{6,4},{8,10},{10,8},{12,14},{14,12},{16,18},{18,... | collective-permute-start | bytes 3145736 | tf_op jit(solution)/shard_map/ppermute | solution.py:441
  103.6 14.3 %collective-permute-start.7 = (bf16[2,128,1024]{2,1,0:T(8,128)(2,1)}, bf16[2,128,1024]{2,1,0:T(8,128)(2,1)}, u32[]{:S(2)}, u32[]{:S(2)}) collective-permute-start(bf16[2,128,1024]{2,1,0:T(8,128)(2,1)} %get-tuple-element.32), channel_id=1, source_target_pairs={{0,1},{1,0},{2,3},{3,2},{4,5},{5,4},{6,7},{7,6},{8,9},{9,8},{10,11... | collective-permute-start | bytes 1572872 | tf_op jit(solution)/shard_map/ppermute | solution.py:419
  104.5 15.1 %collective-permute-start.8 = (bf16[2,128,1024]{2,1,0:T(8,128)(2,1)}, bf16[2,128,1024]{2,1,0:T(8,128)(2,1)}, u32[]{:S(2)}, u32[]{:S(2)}) collective-permute-start(bf16[2,128,1024]{2,1,0:T(8,128)(2,1)} %get-tuple-element.33), channel_id=1, source_target_pairs={{0,4},{2,6},{4,0},{6,2},{8,12},{10,14},{12,8},{14,10},{16,20},{18,... | collective-permute-start | bytes 1572872 | tf_op jit(solution)/shard_map/ppermute | solution.py:420
  106.0 24.3 %collective-permute-start.9 = (bf16[2,128,1024]{2,1,0:T(8,128)(2,1)}, bf16[2,128,1024]{2,1,0:T(8,128)(2,1)}, u32[]{:S(2)}, u32[]{:S(2)}) collective-permute-start(bf16[2,128,1024]{2,1,0:T(8,128)(2,1)} %get-tuple-element.34), channel_id=1, source_target_pairs={{0,5},{1,4},{2,7},{3,6},{4,1},{5,0},{6,3},{7,2},{8,13},{9,12},{10,... | collective-permute-start | bytes 1572872 | tf_op jit(solution)/shard_map/ppermute | solution.py:421
  108.5 48.3 %all-to-all-start.2 = ((bf16[16,128,256]{2,1,0:T(8,128)(2,1)}), bf16[16,128,256]{2,1,0:T(8,128)(2,1)S(1)}, u32[]{:S(2)}, u32[]{:S(2)}) async-start(bf16[16,128,256]{2,1,0:T(8,128)(2,1)} %shard_map.100), calls=%async_computation.2 | async-start | bytes 2097152 | tf_op jit(solution)/shard_map/all_to_all | solution.py:425
  151.3 2.9 %collective-permute-start.14 = (bf16[16,128,256]{2,1,0:T(8,128)(2,1)}, bf16[16,128,256]{2,1,0:T(8,128)(2,1)S(1)}, u32[]{:S(2)}, u32[]{:S(2)}) collective-permute-start(bf16[16,128,256]{2,1,0:T(8,128)(2,1)} %get-tuple-element.43), channel_id=1, source_target_pairs={{0,2},{2,0},{4,6},{6,4},{8,10},{10,8},{12,14},{14,12},{16,18},{18,... | collective-permute-start | bytes 3145736 | tf_op jit(solution)/shard_map/ppermute | solution.py:445
  151.4 26.4 %collective-permute-start.11 = (bf16[2,256,1024]{2,1,0:T(8,128)(2,1)}, bf16[2,256,1024]{2,1,0:T(8,128)(2,1)}, u32[]{:S(2)}, u32[]{:S(2)}) collective-permute-start(bf16[2,256,1024]{2,1,0:T(8,128)(2,1)} %get-tuple-element.36), channel_id=1, source_target_pairs={{0,4},{2,6},{4,0},{6,2},{8,12},{10,14},{12,8},{14,10},{16,20},{18,... | collective-permute-start | bytes 3145736 | tf_op jit(solution)/shard_map/ppermute | solution.py:446
  152.2 47.4 %collective-permute-start.12 = (bf16[2,256,1024]{2,1,0:T(8,128)(2,1)}, bf16[2,256,1024]{2,1,0:T(8,128)(2,1)S(1)}, u32[]{:S(2)}, u32[]{:S(2)}) collective-permute-start(bf16[2,256,1024]{2,1,0:T(8,128)(2,1)} %get-tuple-element.37), channel_id=1, source_target_pairs={{0,4},{2,6},{4,0},{6,2},{8,12},{10,14},{12,8},{14,10},{16,20},{18,... | collective-permute-start | bytes 3145736 | tf_op jit(solution)/shard_map/ppermute | solution.py:446
  154.2 1.2 copy-start
  156.8 46.9 %all-to-all-start.3 = ((bf16[16,128,256]{2,1,0:T(8,128)(2,1)}), bf16[16,128,256]{2,1,0:T(8,128)(2,1)S(1)}, u32[]{:S(2)}, u32[]{:S(2)}) async-start(bf16[16,128,256]{2,1,0:T(8,128)(2,1)} %shard_map.101), calls=%async_computation.3 | async-start | bytes 2097152 | tf_op jit(solution)/shard_map/all_to_all | solution.py:425
  161.5 38.2 %copy-start.5 = (bf16[256,1024]{1,0:T(8,128)(2,1)S(1)}, bf16[256,1024]{1,0:T(8,128)(2,1)}, u32[]{:S(2)}) copy-start(bf16[256,1024]{1,0:T(8,128)(2,1)} %get-tuple-element.31) | copy-start | bytes 1572868
  161.5 38.2 %copy-start.6 = (bf16[256,1024]{1,0:T(8,128)(2,1)S(1)}, bf16[256,1024]{1,0:T(8,128)(2,1)}, u32[]{:S(2)}) copy-start(bf16[256,1024]{1,0:T(8,128)(2,1)} %get-tuple-element.38) | copy-start | bytes 1572868
  161.5 38.2 %copy-start.7 = (bf16[256,1024]{1,0:T(8,128)(2,1)S(1)}, bf16[256,1024]{1,0:T(8,128)(2,1)}, u32[]{:S(2)}) copy-start(bf16[256,1024]{1,0:T(8,128)(2,1)} %get-tuple-element.35) | copy-start | bytes 1572868
  161.5 38.2 %copy-start.8 = (bf16[256,1024]{1,0:T(8,128)(2,1)S(1)}, bf16[256,1024]{1,0:T(8,128)(2,1)}, u32[]{:S(2)}) copy-start(bf16[256,1024]{1,0:T(8,128)(2,1)} %get-tuple-element.39) | copy-start | bytes 1572868
  202.8 6.4 %collective-permute-start.15 = (bf16[2,128,256]{2,1,0:T(8,128)(2,1)S(1)}, bf16[2,128,256]{2,1,0:T(8,128)(2,1)S(1)}, u32[]{:S(2)}, u32[]{:S(2)}) collective-permute-start(bf16[2,128,256]{2,1,0:T(8,128)(2,1)S(1)} %get-tuple-element.49), channel_id=1, source_target_pairs={{0,4},{2,6},{4,0},{6,2},{8,12},{10,14},{12,8},{14,10},{16,20},{18,... | collective-permute-start | bytes 393224 | tf_op jit(solution)/shard_map/ppermute | solution.py:452
  203.9 6.7 %collective-permute-start.16 = (bf16[2,128,256]{2,1,0:T(8,128)(2,1)S(1)}, bf16[2,128,256]{2,1,0:T(8,128)(2,1)S(1)}, u32[]{:S(2)}, u32[]{:S(2)}) collective-permute-start(bf16[2,128,256]{2,1,0:T(8,128)(2,1)S(1)} %get-tuple-element.51), channel_id=1, source_target_pairs={{0,4},{2,6},{4,0},{6,2},{8,12},{10,14},{12,8},{14,10},{16,20},{18,... | collective-permute-start | bytes 393224 | tf_op jit(solution)/shard_map/ppermute | solution.py:452
